TPU v7x, 32 devices: a whole 2x2x4 slice. The times are simulated.
32 devices in a mesh: wide: 8 (over y, x, core), narrow: 4 (over z).
Axes of the slice: x: 2, y: 2, z: 4, core: 2. Of those that a mesh axis runs over, the one named last changes fastest.
Arguments:
- tokens: bfloat16 [64, 128, 1120], P(('wide', 'narrow')), may hold values from -6 to 6
- lengths: int32 [64], P(('wide', 'narrow')), may hold values from 1 to 128, 5120 in all
- ln1_gain: bfloat16 [1120], P('narrow'), may hold values from 0.5 to 1.5
- ln1_bias: bfloat16 [1120], P('narrow'), may hold values from -1 to 1
- w_qkv: bfloat16 [1120, 3360], P('narrow'), may hold values from -0.1875 to 0.1875
- w_out: bfloat16 [1120, 1120], P('narrow'), may hold values from -0.5 to 0.5
- ln2_gain: bfloat16 [1120], P('narrow'), may hold values from 0.5 to 1.5
- ln2_bias: bfloat16 [1120], P('narrow'), may hold values from -1 to 1
- w_fc: bfloat16 [1120, 4480], P('narrow'), may hold values from -0.1875 to 0.1875
- w_proj: bfloat16 [4480, 1120], P('narrow'), may hold values from -0.09375 to 0.09375
- cotangent: bfloat16 [64, 128, 1120], P(('wide', 'narrow')), may hold values from -6 to 6
Outputs:
- result: bfloat16 [64, 128, 1120], P(('wide', 'narrow'))
- grad_tokens: bfloat16 [64, 128, 1120], P(('wide', 'narrow'))
- grad_ln1_gain: float32 [1120], P('narrow')
- grad_ln1_bias: float32 [1120], P('narrow')
- grad_w_qkv: float32 [1120, 3360], P('narrow')
- grad_w_out: float32 [1120, 1120], P('narrow')
- grad_ln2_gain: float32 [1120], P('narrow')
- grad_ln2_bias: float32 [1120], P('narrow')
- grad_w_fc: float32 [1120, 4480], P('narrow')
- grad_w_proj: float32 [4480, 1120], P('narrow')
All inputs are finite; a program needn't handle non-finite values. No bound on the sum of `lengths` on one device may be relied on, other than what follows from the above.
Results may differ from a plain program's by a relative error of at most 0.015.
Values may be sent and summed in bfloat16 or wider, within the bound.
A program may use at most 256 MiB of HBM per device.

v0:
```python
from functools import partial

import jax
import jax.numpy as jnp
from jax import lax
from jax.sharding import PartitionSpec as P

HEADS = 20


EPS = 1e-05
MASKED = -1e30


def layer_norm(in_rows, gain_vec, shift_vec):
    row_mean = jnp.mean(in_rows, axis=-1, keepdims=True)
    centered = in_rows - row_mean
    inv_std = lax.rsqrt(jnp.mean(centered * centered, axis=-1, keepdims=True) + EPS)
    normed = centered * inv_std
    return (normed * gain_vec + shift_vec, normed, inv_std)


def norm_grad(grad_rows, gain_vec, normed, inv_std):
    scaled = grad_rows * gain_vec
    return inv_std * (
        scaled
        - jnp.mean(scaled, axis=-1, keepdims=True)
        - normed * jnp.mean(scaled * normed, axis=-1, keepdims=True)
    )


def inner_rows(left, right):
    return lax.dot_general(
        left, right, (((0,), (0,)), ((), ())), preferred_element_type=jnp.float32
    )


def times_trans(left, right):
    return lax.dot_general(
        left, right, (((1,), (1,)), ((), ())), preferred_element_type=jnp.float32
    )


def attn_scores(queries, key_rows, length):
    seq_len = queries.shape[0]
    head_size = queries.shape[2]
    scores = jnp.einsum(
        "qhd,khd->hqk", queries, key_rows, preferred_element_type=jnp.float32
    ) * head_size ** (-0.5)
    query_pos = lax.broadcasted_iota(jnp.int32, (seq_len, seq_len), 0)
    key_pos = lax.broadcasted_iota(jnp.int32, (seq_len, seq_len), 1)
    allowed = (key_pos <= query_pos) & (key_pos < length)
    return jnp.where(allowed[None], scores, MASKED)


def forward_cell(in_rows, length, weights):
    gain_one, shift_one, weight_qkv, weight_out, gain_two, shift_two, weight_fc, weight_proj = (
        weights
    )
    seq_len, model_width = in_rows.shape
    head_size = model_width // HEADS
    first_norm, normed_one, inv_one = layer_norm(
        in_rows, gain_one.astype(jnp.float32), shift_one.astype(jnp.float32)
    )
    first_low = first_norm.astype(jnp.bfloat16)
    projected = jnp.dot(first_low, weight_qkv, preferred_element_type=jnp.float32)
    queries = projected[:, :model_width].astype(jnp.bfloat16).reshape(seq_len, HEADS, head_size)
    key_rows = (
        projected[:, model_width : 2 * model_width]
        .astype(jnp.bfloat16)
        .reshape(seq_len, HEADS, head_size)
    )
    value_rows = (
        projected[:, 2 * model_width :].astype(jnp.bfloat16).reshape(seq_len, HEADS, head_size)
    )
    scores = attn_scores(queries, key_rows, length)
    row_max = jnp.max(scores, axis=-1, keepdims=True)
    exp_scores = jnp.exp(scores - row_max)
    row_total = jnp.sum(exp_scores, axis=-1, keepdims=True)
    attn_prob = exp_scores / row_total
    log_total = row_max + jnp.log(row_total)
    heads_out = jnp.einsum(
        "hqk,khd->qhd",
        attn_prob.astype(jnp.bfloat16),
        value_rows,
        preferred_element_type=jnp.float32,
    )
    attended = heads_out.reshape(seq_len, model_width).astype(jnp.bfloat16)
    mixed_rows = in_rows + jnp.dot(attended, weight_out, preferred_element_type=jnp.float32)
    second_norm, normed_two, inv_two = layer_norm(
        mixed_rows, gain_two.astype(jnp.float32), shift_two.astype(jnp.float32)
    )
    second_low = second_norm.astype(jnp.bfloat16)
    pre_act = jnp.dot(second_low, weight_fc, preferred_element_type=jnp.float32)
    gelu_out = jax.nn.gelu(pre_act, approximate=True).astype(jnp.bfloat16)
    result = mixed_rows + jnp.dot(gelu_out, weight_proj, preferred_element_type=jnp.float32)
    saved_acts = (
        normed_one,
        inv_one,
        first_low,
        queries,
        key_rows,
        value_rows,
        log_total,
        attended,
        normed_two,
        inv_two,
        second_low,
        pre_act,
        gelu_out,
    )
    return (result, saved_acts)


def backward_cell(grad_rows, length, saved_acts, weights):
    gain_one, shift_one, weight_qkv, weight_out, gain_two, shift_two, weight_fc, weight_proj = (
        weights
    )
    (
        normed_one,
        inv_one,
        first_low,
        queries,
        key_rows,
        value_rows,
        log_total,
        attended,
        normed_two,
        inv_two,
        second_low,
        pre_act,
        gelu_out,
    ) = saved_acts
    seq_len, model_width = grad_rows.shape
    head_size = model_width // HEADS
    grad_low = grad_rows.astype(jnp.bfloat16)
    grad_wproj = inner_rows(gelu_out, grad_low)
    grad_gelu = times_trans(grad_low, weight_proj)
    unused, gelu_pull = jax.vjp(partial(jax.nn.gelu, approximate=True), pre_act)
    grad_pre = gelu_pull(grad_gelu)[0].astype(jnp.bfloat16)
    grad_wfc = inner_rows(second_low, grad_pre)
    grad_second = times_trans(grad_pre, weight_fc)
    grad_gain_two = jnp.sum(grad_second * normed_two, axis=0)
    grad_shift_two = jnp.sum(grad_second, axis=0)
    grad_mixed = grad_rows + norm_grad(
        grad_second, gain_two.astype(jnp.float32), normed_two, inv_two
    )
    mixed_low = grad_mixed.astype(jnp.bfloat16)
    grad_wout = inner_rows(attended, mixed_low)
    grad_attended = (
        times_trans(mixed_low, weight_out).astype(jnp.bfloat16).reshape(seq_len, HEADS, head_size)
    )
    scores = attn_scores(queries, key_rows, length)
    attn_prob = jnp.exp(scores - log_total)
    grad_value = jnp.einsum(
        "hqk,qhd->khd",
        attn_prob.astype(jnp.bfloat16),
        grad_attended,
        preferred_element_type=jnp.float32,
    )
    grad_prob = jnp.einsum(
        "qhd,khd->hqk", grad_attended, value_rows, preferred_element_type=jnp.float32
    )
    grad_scores = attn_prob * (grad_prob - jnp.sum(attn_prob * grad_prob, axis=-1, keepdims=True))
    grad_scores = grad_scores.astype(jnp.bfloat16)
    scale_factor = head_size ** (-0.5)
    grad_query = (
        jnp.einsum("hqk,khd->qhd", grad_scores, key_rows, preferred_element_type=jnp.float32)
        * scale_factor
    )
    grad_key = (
        jnp.einsum("hqk,qhd->khd", grad_scores, queries, preferred_element_type=jnp.float32)
        * scale_factor
    )
    grad_proj_in = jnp.concatenate(
        [
            grad_query.reshape(seq_len, model_width),
            grad_key.reshape(seq_len, model_width),
            grad_value.reshape(seq_len, model_width),
        ],
        axis=1,
    ).astype(jnp.bfloat16)
    grad_wqkv = inner_rows(first_low, grad_proj_in)
    grad_first = times_trans(grad_proj_in, weight_qkv)
    grad_gain_one = jnp.sum(grad_first * normed_one, axis=0)
    grad_shift_one = jnp.sum(grad_first, axis=0)
    grad_input = grad_mixed + norm_grad(
        grad_first, gain_one.astype(jnp.float32), normed_one, inv_one
    )
    grads = (
        grad_gain_one,
        grad_shift_one,
        grad_wqkv,
        grad_wout,
        grad_gain_two,
        grad_shift_two,
        grad_wfc,
        grad_wproj,
    )
    return (grads, grad_input)


def shards(
    tokens, lengths, ln1_gain, ln1_bias, w_qkv, w_out, ln2_gain, ln2_bias, w_fc, w_proj, cotangent
):
    outputs = []
    input_grads = []
    running = None
    held = None
    held = (
        lax.all_gather(ln1_gain, "narrow", axis=0, tiled=True),
        lax.all_gather(ln1_bias, "narrow", axis=0, tiled=True),
        lax.all_gather(w_qkv, "narrow", axis=0, tiled=True),
        lax.all_gather(w_out, "narrow", axis=0, tiled=True),
        lax.all_gather(ln2_gain, "narrow", axis=0, tiled=True),
        lax.all_gather(ln2_bias, "narrow", axis=0, tiled=True),
        lax.all_gather(w_fc, "narrow", axis=0, tiled=True),
        lax.all_gather(w_proj, "narrow", axis=0, tiled=True),
    )
    for micro_step in range(tokens.shape[0]):
        in_rows = tokens[micro_step].astype(jnp.float32)
        result, saved_acts = forward_cell(in_rows, lengths[micro_step], held)
        grads, grad_input = backward_cell(
            cotangent[micro_step].astype(jnp.float32), lengths[micro_step], saved_acts, held
        )
        grads = (
            lax.psum_scatter(
                grads[0].astype(jnp.bfloat16), "narrow", scatter_dimension=0, tiled=True
            ).astype(jnp.float32),
            lax.psum_scatter(
                grads[1].astype(jnp.bfloat16), "narrow", scatter_dimension=0, tiled=True
            ).astype(jnp.float32),
            lax.psum_scatter(
                grads[2].astype(jnp.bfloat16), "narrow", scatter_dimension=0, tiled=True
            ).astype(jnp.float32),
            lax.psum_scatter(
                grads[3].astype(jnp.bfloat16), "narrow", scatter_dimension=0, tiled=True
            ).astype(jnp.float32),
            lax.psum_scatter(
                grads[4].astype(jnp.bfloat16), "narrow", scatter_dimension=0, tiled=True
            ).astype(jnp.float32),
            lax.psum_scatter(
                grads[5].astype(jnp.bfloat16), "narrow", scatter_dimension=0, tiled=True
            ).astype(jnp.float32),
            lax.psum_scatter(
                grads[6].astype(jnp.bfloat16), "narrow", scatter_dimension=0, tiled=True
            ).astype(jnp.float32),
            lax.psum_scatter(
                grads[7].astype(jnp.bfloat16), "narrow", scatter_dimension=0, tiled=True
            ).astype(jnp.float32),
        )
        if running is None:
            running = tuple(grads)
        else:
            running = jax.tree.map(jnp.add, running, tuple(grads))
        outputs.append(result.astype(jnp.bfloat16))
        input_grads.append(grad_input.astype(jnp.bfloat16))
    totals = lax.psum(
        (
            running[0],
            running[1],
            running[2],
            running[3],
            running[4],
            running[5],
            running[6],
            running[7],
        ),
        "wide",
    )
    return (
        jnp.stack(outputs),
        jnp.stack(input_grads),
        totals[0],
        totals[1],
        totals[2],
        totals[3],
        totals[4],
        totals[5],
        totals[6],
        totals[7],
    )


def solution(mesh):
    placed = (
        P(("wide", "narrow"), None, None),
        P(("wide", "narrow")),
        P("narrow"),
        P("narrow"),
        P("narrow", None),
        P("narrow", None),
        P("narrow"),
        P("narrow"),
        P("narrow", None),
        P("narrow", None),
        P(("wide", "narrow"), None, None),
    )
    return jax.shard_map(
        shards,
        mesh=mesh,
        in_specs=placed,
        out_specs=(
            P(("wide", "narrow"), None, None),
            P(("wide", "narrow"), None, None),
            P("narrow"),
            P("narrow"),
            P("narrow", None),
            P("narrow", None),
            P("narrow"),
            P("narrow"),
            P("narrow", None),
            P("narrow", None),
        ),
        check_vma=False,
    )
```

profile of v0, /device:TPU:0, one launch (start us, length us, event | category | flops | bytes accessed | tf_op | source)
XLA Modules:
  0.0 1940.0 jit_solution(7054452159979737081)
XLA Ops:
  7.2 0.7 all-gather.5.cloned.1.call-update
  8.0 0.7 all-gather.7.cloned.1.call-update
  8.8 0.7 all-gather.9.cloned.1.call-update
  12.4 21.1 %all-reduce.21 = (bf16[1120]{0:T(1024)(128)(2,1)S(1)}, bf16[1120]{0:T(1024)(128)(2,1)S(1)}, bf16[1120]{0:T(1024)(128)(2,1)S(1)}, bf16[1120]{0:T(1024)(128)(2,1)S(1)}) all-reduce(bf16[1120]{0:T(1024)(128)(2,1)S(1)} %dynamic-update-slice.1, bf16[1120]{0:T(1024)(128)(2,1)S(1)} %dynamic-update-slice, ...), channel_id=1, replica_groups=mesh['wide'=8,'narrow'=4] {'narrow'}, use_global_device_ids=true, to_apply=%add.1 | all-reduce | flops 4480 | bytes 17920
  36.0 115.5 %all-gather.5.cloned.1.call-done = bf16[1120,3360]{1,0:T(8,128)(2,1)} async-done(((bf16[280,3360]{1,0:T(8,128)(2,1)}), bf16[1120,3360]{1,0:T(8,128)(2,1)}) %all-gather.5.cloned.1.call-update) | async-done | bytes 7526416 | tf_op jit(solution)/shard_map/all_gather | solution.py:213
  151.5 6.6 convolution_convert_fusion.9
  158.9 0.8 copy-done.4
  160.1 45.2 %all-gather.7.cloned.1.call-done = bf16[1120,1120]{1,0:T(8,128)(2,1)} async-done(((bf16[280,1120]{1,0:T(8,128)(2,1)}), bf16[1120,1120]{1,0:T(8,128)(2,1)}) %all-gather.7.cloned.1.call-update) | async-done | bytes 2508816 | tf_op jit(solution)/shard_map/all_gather | solution.py:214
  205.3 2.8 fusion.105
  208.3 6.6 convolution_convert_fusion.8
  216.5 1.5 copy-done.1
  218.1 1.1 fusion.103
  219.3 0.8 copy-done.6
  220.2 162.0 %all-gather.9.cloned.1.call-done = bf16[1120,4480]{1,0:T(8,128)(2,1)} async-done(((bf16[280,4480]{1,0:T(8,128)(2,1)}), bf16[1120,4480]{1,0:T(8,128)(2,1)}) %all-gather.9.cloned.1.call-update) | async-done | bytes 10035216 | tf_op jit(solution)/shard_map/all_gather | solution.py:217
  382.2 7.6 fusion.97
  389.9 173.2 %all-gather.11.cloned.1.call-done = bf16[4480,1120]{1,0:T(8,128)(2,1)} async-done(((bf16[1120,1120]{1,0:T(8,128)(2,1)}), bf16[4480,1120]{1,0:T(8,128)(2,1)}) %all-gather.11.cloned.1.call-update) | async-done | bytes 10035216 | tf_op jit(solution)/shard_map/all_gather | solution.py:218
  563.1 8.1 fusion.17
  571.3 1.0 copy-done.22
  572.3 2.8 fusion.106
  575.1 1.9 fusion.96
  577.0 8.1 fusion.10
  585.1 3.9 multiply_reduce_fusion.3
  589.1 1.2 multiply_add_fusion.1
  590.3 0.8 copy-done.18
  591.1 2.3 convolution_convert_fusion.6
  593.5 3.5 convolution_convert_fusion.7
  597.1 2.1 convolution_convert_fusion.11
  602.9 4.6 convolution_convert_fusion.5
  607.6 2.0 convolution_convert_fusion.10
  612.6 0.7 copy-done.50
  613.3 4.7 convolution_convert_fusion.4
  618.4 1.4 copy-done.15
  619.7 7.8 convolution_convert_fusion.1
  627.6 1.6 copy-done.13
  629.2 7.9 convolution_convert_fusion
  637.1 1.0 copy-done.8
  638.5 5.6 convolution_convert_fusion.2
  644.2 1.2 copy-done.21
  645.4 5.6 convolution_convert_fusion.3
  651.1 45.7 %reduce-scatter.29.cloned.1.call-done = bf16[280,1120]{1,0:T(8,128)(2,1)} async-done(((bf16[1120,1120]{1,0:T(8,128)(2,1)}), bf16[280,1120]{1,0:T(8,128)(2,1)}) %reduce-scatter.29.cloned.1.call-update) | async-done | bytes 627216
  696.7 2.5 convert_add_fusion.3
  699.2 134.6 %reduce-scatter.25.cloned.1.call-done = bf16[280,3360]{1,0:T(8,128)(2,1)} async-done(((bf16[1120,3360]{1,0:T(8,128)(2,1)}), bf16[280,3360]{1,0:T(8,128)(2,1)}) %reduce-scatter.25.cloned.1.call-update) | async-done | bytes 1881616
  833.8 137.3 %reduce-scatter.27.cloned.1.call-done = bf16[280,3360]{1,0:T(8,128)(2,1)} async-done(((bf16[1120,3360]{1,0:T(8,128)(2,1)}), bf16[280,3360]{1,0:T(8,128)(2,1)}) %reduce-scatter.27.cloned.1.call-update) | async-done | bytes 1881616
  971.1 4.4 convert_add_fusion.2
  975.5 174.1 %reduce-scatter.21.cloned.1.call-done = bf16[1120,1120]{1,0:T(8,128)(2,1)} async-done(((bf16[4480,1120]{1,0:T(8,128)(2,1)}), bf16[1120,1120]{1,0:T(8,128)(2,1)}) %reduce-scatter.21.cloned.1.call-update) | async-done | bytes 2508816 | tf_op jit(solution)/shard_map/reduce_scatter | solution.py:248
  1149.7 179.0 %reduce-scatter.23.cloned.1.call-done = bf16[1120,1120]{1,0:T(8,128)(2,1)} async-done(((bf16[4480,1120]{1,0:T(8,128)(2,1)}), bf16[1120,1120]{1,0:T(8,128)(2,1)}) %reduce-scatter.23.cloned.1.call-update) | async-done | bytes 2508816 | tf_op jit(solution)/shard_map/reduce_scatter | solution.py:248
  1328.7 5.3 convert_add_fusion
  1334.0 184.3 %reduce-scatter.35.cloned.1.call-done = bf16[280,4480]{1,0:T(8,128)(2,1)} async-done(((bf16[1120,4480]{1,0:T(8,128)(2,1)}), bf16[280,4480]{1,0:T(8,128)(2,1)}) %reduce-scatter.35.cloned.1.call-update) | async-done | bytes 2508816
  1518.3 189.9 %reduce-scatter.33.cloned.1.call-done = bf16[280,4480]{1,0:T(8,128)(2,1)} async-done(((bf16[1120,4480]{1,0:T(8,128)(2,1)}), bf16[280,4480]{1,0:T(8,128)(2,1)}) %reduce-scatter.33.cloned.1.call-update) | async-done | bytes 2508816
  1708.3 5.2 convert_add_fusion.1
  1714.7 5.5 fusion.65
  1720.2 5.8 fusion.53
  1726.0 22.8 %all-reduce.20 = (bf16[1120]{0:T(1024)(128)(2,1)S(1)}, bf16[1120]{0:T(1024)(128)(2,1)S(1)}, bf16[1120]{0:T(1024)(128)(2,1)S(1)}, bf16[1120]{0:T(1024)(128)(2,1)S...) all-reduce(bf16[1120]{0:T(1024)(128)(2,1)S(1)} %get-tuple-element.1, ...), channel_id=3, replica_groups=mesh['wide'=8,'narrow'=4] {'narrow'}, use_global_device_ids=true, to_apply=%region_25.26.clone | all-reduce | flops 8960 | bytes 35840
  1749.2 14.1 all-reduce.18
  1763.3 9.1 fusion.2
  1772.5 8.3 fusion.3
  1780.8 0.9 pad_maximum_fusion.2
  1782.1 0.9 pad_maximum_fusion.3
  1783.0 138.6 %all-reduce.24.cloned.1.call-done = (f32[280,3360]{1,0:T(8,128)}, f32[280,1120]{1,0:T(8,128)}, f32[280,4480]{1,0:T(8,128)}, f32[1120,1120]{1,0:T(8,128)}) async-done(((f32[280,3360]{1,0:T(8,128)}, f32[280,1120]{1,0:T(8,128)}, f32[280,4480]{1,0:T(8,128)}, f32[1120,1120]{1,0:T(8,128)}), (f32[280,3360]{1,0:T(8,128)}, f32[280,1120]{1,0:T(8,128)}, f32[280,4480]{1,0:T(8,128)}, ...) | async-done | bytes 15052816 | tf_op jit(solution)/shard_map/psum | solution.py:258
  1921.5 4.4 copy.53
  1925.9 1.0 copy.54
  1927.0 2.6 copy.55
  1929.5 0.7 slice-done
  1930.7 2.3 copy.56
  (208 shorter events, 17.2 us)
Async XLA Ops:
  7.2 144.3 %all-gather.5.cloned.1.call-start = ((), (), s32[]{:S(2)}) async-start(), calls=%async_computation.8 | async-start | bytes 9676800 | tf_op jit(solution)/shard_map/all_gather | solution.py:213
  7.9 197.4 %all-gather.7.cloned.1.call-start = ((), (), s32[]{:S(2)}) async-start(), calls=%async_computation.9 | async-start | bytes 3225600 | tf_op jit(solution)/shard_map/all_gather | solution.py:214
  8.7 1.4 copy-start.58
  8.7 2.7 copy-start.60
  8.7 2.9 copy-start.61
  8.7 3.2 copy-start.62
  8.7 3.4 copy-start.63
  8.7 24.8 %copy-start.59 = (s32[2]{0:T(128)S(1)}, s32[2]{0:T(128)}, u32[]{:S(2)}) copy-start(s32[2]{0:T(128)} %param.12) | copy-start | bytes 28
  8.7 26.7 %copy-start.9 = (bf16[2,128,1120]{1,2,0:T(8,128)(2,1)S(1)}, bf16[2,128,1120]{1,2,0:T(8,128)(2,1)}, u32[]{:S(2)}) copy-start(bf16[2,128,1120]{1,2,0:T(8,128)(2,1)} %param.11) | copy-start | bytes 1720324
  8.7 373.5 %all-gather.9.cloned.1.call-start = ((), (), s32[]{:S(2)}) async-start(), calls=%async_computation.10 | async-start | bytes 12544000 | tf_op jit(solution)/shard_map/all_gather | solution.py:217
  9.5 553.6 %all-gather.11.cloned.1.call-start = ((), (), s32[]{:S(2)}) async-start(), calls=%async_computation.11 | async-start | bytes 12902400 | tf_op jit(solution)/shard_map/all_gather | solution.py:218
  10.0 641.0 %reduce-scatter.31.cloned.1.call-start = ((), (), s32[]{:S(2)}) async-start(), calls=%async_computation.17 | async-start | bytes 3225600
  35.8 122.3 %copy-start.54 = (f32[128]{0:T(128)}, f32[128]{0:T(128)S(1)}, u32[]{:S(2)}) copy-start(f32[128]{0:T(128)S(1)} %add_rsqrt_fusion.3) | copy-start | bytes 1540
  35.8 172.5 %copy-start.56 = (f32[128]{0:T(128)}, f32[128]{0:T(128)S(1)}, u32[]{:S(2)}) copy-start(f32[128]{0:T(128)S(1)} %add_rsqrt_fusion.1) | copy-start | bytes 1540
  158.2 1.9 copy-start.27
  158.2 1.9 copy-start.29
  158.6 1.1 copy-start.4
  160.1 54.9 %copy-start.37 = (bf16[20,56,128]{2,1,0:T(8,128)(2,1)}, bf16[20,56,128]{2,1,0:T(8,128)(2,1)S(1)}, u32[]{:S(2)}) copy-start(bf16[20,56,128]{2,1,0:T(8,128)(2,1)S(1)} %convolution_convert_fusion.15) | copy-start | bytes 860164
  215.7 2.3 copy-start.1
  215.7 2.5 copy-start.10
  216.5 3.7 copy-start.38
  563.1 9.2 copy-start
  575.1 1.9 copy-start.31
  576.9 8.1 copy-start.14
  577.0 8.1 copy-start.7
  585.1 3.9 copy-start.20
  589.0 2.1 copy-start.39
  593.5 103.3 %reduce-scatter.29.cloned.1.call-start = ((), (), s32[]{:S(2)}) async-start(), calls=%async_computation.16 | async-start | bytes 3225600
  597.0 236.8 %reduce-scatter.25.cloned.1.call-start = ((), (), s32[]{:S(2)}) async-start(), calls=%async_computation.14 | async-start | bytes 9676800
  597.1 2.2 copy-start.5
  597.1 2.2 copy-start.36
  599.7 1.5 copy-start.28
  600.7 2.2 copy-start.11
  600.7 2.2 copy-start.55
  607.5 363.6 %reduce-scatter.27.cloned.1.call-start = ((), (), s32[]{:S(2)}) async-start(), calls=%async_computation.15 | async-start | bytes 9676800
  607.6 2.0 copy-start.3
  607.6 2.0 copy-start.34
  611.1 2.2 copy-start.12
  611.1 2.2 copy-start.57
  611.7 6.4 copy-start.44
  612.0 6.1 copy-start.46
  618.1 1.6 copy-start.15
  618.1 531.6 %reduce-scatter.21.cloned.1.call-start = ((), (), s32[]{:S(2)}) async-start(), calls=%async_computation.12 | async-start | bytes 12902400 | tf_op jit(solution)/shard_map/reduce_scatter | solution.py:248
  627.5 1.6 copy-start.13
  627.5 701.2 %reduce-scatter.23.cloned.1.call-start = ((), (), s32[]{:S(2)}) async-start(), calls=%async_computation.13 | async-start | bytes 12902400 | tf_op jit(solution)/shard_map/reduce_scatter | solution.py:248
  637.0 1.1 copy-start.8
  637.0 1.5 copy-start.23
  637.1 881.3 %reduce-scatter.35.cloned.1.call-start = ((), (), s32[]{:S(2)}) async-start(), calls=%async_computation.19 | async-start | bytes 12544000
  644.1 1.3 copy-start.21
  644.1 1064.2 %reduce-scatter.33.cloned.1.call-start = ((), (), s32[]{:S(2)}) async-start(), calls=%async_computation.18 | async-start | bytes 12544000
  651.0 1270.5 %all-reduce.24.cloned.1.call-start = ((), (), s32[]{:S(2)}) async-start(), calls=%async_computation.20 | async-start | bytes 30679040 | tf_op jit(solution)/shard_map/psum | solution.py:258
  1713.5 1.1 copy-start.49
  1714.7 5.5 copy-start.45
  1714.7 5.5 copy-start.47
  1714.7 5.5 copy-start.51
  1720.2 5.8 copy-start.52
  1720.2 5.8 copy-start.53
  1763.3 9.1 copy-start.16
  1772.5 9.2 copy-start.17
  1772.5 9.2 copy-start.19
  1921.5 4.4 copy-start.32
  1921.5 5.5 copy-start.24
  1925.9 4.3 slice-start
  1927.0 3.7 slice-start.1
  (15 other events, 13.6 us)
Sparse Core Ops, SparseCore 0:
  9.6 141.9 all-gather.4
  153.1 52.2 all-gather.6
  206.9 175.2 all-gather.8
  383.7 179.3 all-gather.10
  593.6 49.2 reduce-scatter.30
  645.6 51.1 reduce-scatter.28
  699.0 134.7 reduce-scatter.24
  836.1 134.9 reduce-scatter.26
  973.5 176.0 reduce-scatter.20
  1151.9 176.7 reduce-scatter.22
  1331.1 187.2 reduce-scatter.34
  1520.6 187.6 reduce-scatter.32
  1713.7 207.8 all-reduce.23
where the time goes:
time: 1950 us; the launch traced here: 1940 us
  waiting for transfers between devices  1680 us (86%)
  matrix products  130 us (7%)
  blocking collectives  58 us (3%)
  local copies, waits for them, and re-layouts  28 us (1%)
  other arithmetic  24.4 us (1%)
    unnamed x19, waiting for transfers between devices  695 us
    reduce_scatter x2, waiting for transfers between devices, shards(): lax.psum_scatter(grads[7].astype(jnp.bfloat16), 'narrow', scatter_dimensi...  353 us
    all_gather x1, waiting for transfers between devices, shards(): lax.all_gather(w_proj, 'narrow', axis=0, tiled=True)  173 us
    all_gather x1, waiting for transfers between devices, shards(): lax.all_gather(w_fc, 'narrow', axis=0, tiled=True)  162 us
    psum x1, waiting for transfers between devices, shards(): lax.psum((running[0], running[1], running[2], running[3], running[4], run...  139 us
    all_gather x1, waiting for transfers between devices, shards(): lax.all_gather(w_qkv, 'narrow', axis=0, tiled=True)  116 us
    all_gather x1, waiting for transfers between devices, shards(): lax.all_gather(w_out, 'narrow', axis=0, tiled=True)  45.2 us
    unnamed x2, blocking collectives  43.9 us
  transfers between devices with their start and end apart: 13, of which 12 were waited for; matrix products, arithmetic and copies ran while one was open for 6% of the time, Pallas kernels for 0%

commit v1 on v0

--- a/solution.py
+++ b/solution.py
@@ -223,51 +223,19 @@
         grads, grad_input = backward_cell(
             cotangent[micro_step].astype(jnp.float32), lengths[micro_step], saved_acts, held
         )
-        grads = (
-            lax.psum_scatter(
-                grads[0].astype(jnp.bfloat16), "narrow", scatter_dimension=0, tiled=True
-            ).astype(jnp.float32),
-            lax.psum_scatter(
-                grads[1].astype(jnp.bfloat16), "narrow", scatter_dimension=0, tiled=True
-            ).astype(jnp.float32),
-            lax.psum_scatter(
-                grads[2].astype(jnp.bfloat16), "narrow", scatter_dimension=0, tiled=True
-            ).astype(jnp.float32),
-            lax.psum_scatter(
-                grads[3].astype(jnp.bfloat16), "narrow", scatter_dimension=0, tiled=True
-            ).astype(jnp.float32),
-            lax.psum_scatter(
-                grads[4].astype(jnp.bfloat16), "narrow", scatter_dimension=0, tiled=True
-            ).astype(jnp.float32),
-            lax.psum_scatter(
-                grads[5].astype(jnp.bfloat16), "narrow", scatter_dimension=0, tiled=True
-            ).astype(jnp.float32),
-            lax.psum_scatter(
-                grads[6].astype(jnp.bfloat16), "narrow", scatter_dimension=0, tiled=True
-            ).astype(jnp.float32),
-            lax.psum_scatter(
-                grads[7].astype(jnp.bfloat16), "narrow", scatter_dimension=0, tiled=True
-            ).astype(jnp.float32),
-        )
-        if running is None:
-            running = tuple(grads)
-        else:
-            running = jax.tree.map(jnp.add, running, tuple(grads))
+        running = grads if running is None else jax.tree.map(jnp.add, running, grads)
         outputs.append(result.astype(jnp.bfloat16))
         input_grads.append(grad_input.astype(jnp.bfloat16))
-    totals = lax.psum(
-        (
-            running[0],
-            running[1],
-            running[2],
-            running[3],
-            running[4],
-            running[5],
-            running[6],
-            running[7],
-        ),
-        "wide",
-    )
+    totals = []
+    for grad in running:
+        part = lax.psum_scatter(
+            grad.astype(jnp.bfloat16), "narrow", scatter_dimension=0, tiled=True
+        )
+        if part.ndim == 2:
+            part = lax.psum(part, "wide").astype(jnp.float32)
+        else:
+            part = lax.psum(part.astype(jnp.float32), "wide")
+        totals.append(part)
     return (
         jnp.stack(outputs),
         jnp.stack(input_grads),

time: 1950 us -> 1300 us (0.67)
  waiting for transfers between devices: 1680 us -> 1040 us
    unnamed x19 -> x12, waiting for transfers between devices: 695 us -> 269 us
    reduce_scatter x2 -> x1, waiting for transfers between devices: 353 us -> 182 us  [shards(): lax.psum_scatter(grad.astype(jnp.bfloat16), 'narrow', scatter_dimension=0...]
    psum x1, waiting for transfers between devices: 139 us -> 90.5 us  [shards(): part = lax.psum(part, 'wide').astype(jnp.float32)]
    dot_general x8, matrix products: 42 us -> 64.1 us  [inner_rows(): lax.dot_general(left, right, (((0,), (0,)), ((), ())), preferred_element_...]
  transfers between devices with their start and end apart: 13 -> 9, of which waited for: 12 -> 8; matrix products, arithmetic and copies ran while one was open for 6% -> 10% of each run, Pallas kernels for 0% -> 0%
where the time goes in v1:
time: 1300 us; the launch traced here: 1290 us
  waiting for transfers between devices  1040 us (80%)
  matrix products  148 us (11%)
  blocking collectives  57.2 us (4%)
  other arithmetic  19.2 us (1%)
  between operations  17 us (1%)
  local copies, waits for them, and re-layouts  13.7 us (1%)
    unnamed x12, waiting for transfers between devices  269 us
    reduce_scatter x1, waiting for transfers between devices, shards(): lax.psum_scatter(grad.astype(jnp.bfloat16), 'narrow', scatter_dimension=0...  182 us
    all_gather x1, waiting for transfers between devices, shards(): lax.all_gather(w_proj, 'narrow', axis=0, tiled=True)  173 us
    all_gather x1, waiting for transfers between devices, shards(): lax.all_gather(w_fc, 'narrow', axis=0, tiled=True)  161 us
    all_gather x1, waiting for transfers between devices, shards(): lax.all_gather(w_qkv, 'narrow', axis=0, tiled=True)  116 us
    psum x1, waiting for transfers between devices, shards(): part = lax.psum(part, 'wide').astype(jnp.float32)  90.5 us
    dot_general x8, matrix products, inner_rows(): lax.dot_general(left, right, (((0,), (0,)), ((), ())), preferred_element_...  64.1 us
    all_gather x1, waiting for transfers between devices, shards(): lax.all_gather(w_out, 'narrow', axis=0, tiled=True)  45.3 us
  transfers between devices with their start and end apart: 9, of which 8 were waited for; matrix products, arithmetic and copies ran while one was open for 10% of the time, Pallas kernels for 0%

profile of v1, /device:TPU:0, one launch (start us, length us, event | category | flops | bytes accessed | tf_op | source)
XLA Modules:
  0.0 1292.5 jit_solution(16745767182800808506)
XLA Ops:
  7.2 0.7 all-gather.5.cloned.1.call-update
  8.0 0.7 all-gather.7.cloned.1.call-update
  8.8 0.7 all-gather.9.cloned.1.call-update
  10.1 0.6 fusion.108
  12.4 21.1 %all-reduce.14 = (bf16[1120]{0:T(1024)(128)(2,1)S(1)}, bf16[1120]{0:T(1024)(128)(2,1)S(1)}, bf16[1120]{0:T(1024)(128)(2,1)S(1)}, bf16[1120]{0:T(1024)(128)(2,1)S(1)}) all-reduce(bf16[1120]{0:T(1024)(128)(2,1)S(1)} %dynamic-update-slice.1, bf16[1120]{0:T(1024)(128)(2,1)S(1)} %dynamic-update-slice, ...), channel_id=1, replica_groups=mesh['wide'=8,'narrow'=4] {'narrow'}, use_global_device_ids=true, to_apply=%add.1 | all-reduce | flops 4480 | bytes 17920
  33.5 0.6 fusion.109
  34.1 0.6 iota_compare_fusion.2
  34.8 0.7 iota_compare_fusion.1
  36.0 115.5 %all-gather.5.cloned.1.call-done = bf16[1120,3360]{1,0:T(8,128)(2,1)} async-done(((bf16[280,3360]{1,0:T(8,128)(2,1)}), bf16[1120,3360]{1,0:T(8,128)(2,1)}) %all-gather.5.cloned.1.call-update) | async-done | bytes 7526416 | tf_op jit(solution)/shard_map/all_gather | solution.py:213
  151.5 6.6 convolution_convert_fusion.1
  158.8 0.8 copy-done.2
  160.1 45.3 %all-gather.7.cloned.1.call-done = bf16[1120,1120]{1,0:T(8,128)(2,1)} async-done(((bf16[280,1120]{1,0:T(8,128)(2,1)}), bf16[1120,1120]{1,0:T(8,128)(2,1)}) %all-gather.7.cloned.1.call-update) | async-done | bytes 2508816 | tf_op jit(solution)/shard_map/all_gather | solution.py:214
  205.3 2.8 fusion.113
  208.4 6.6 convolution_convert_fusion
  216.5 1.5 copy-done.1
  218.2 1.1 fusion.111
  219.4 0.8 copy-done.8
  220.9 161.4 %all-gather.9.cloned.1.call-done = bf16[1120,4480]{1,0:T(8,128)(2,1)} async-done(((bf16[280,4480]{1,0:T(8,128)(2,1)}), bf16[1120,4480]{1,0:T(8,128)(2,1)}) %all-gather.9.cloned.1.call-update) | async-done | bytes 10035216 | tf_op jit(solution)/shard_map/all_gather | solution.py:217
  382.2 7.6 fusion.105
  389.9 173.2 %all-gather.11.cloned.1.call-done = bf16[4480,1120]{1,0:T(8,128)(2,1)} async-done(((bf16[1120,1120]{1,0:T(8,128)(2,1)}), bf16[4480,1120]{1,0:T(8,128)(2,1)}) %all-gather.11.cloned.1.call-update) | async-done | bytes 10035216 | tf_op jit(solution)/shard_map/all_gather | solution.py:218
  563.1 8.1 fusion.21
  571.3 1.0 copy-done.28
  572.3 2.8 fusion.114
  575.1 1.9 fusion.104
  577.0 8.1 fusion.14
  585.1 3.9 multiply_reduce_fusion.3
  590.0 0.8 fusion.90
  591.0 2.3 fusion.3
  593.4 2.0 convolution_convert_fusion.2
  596.3 0.6 copy-done.35
  596.9 0.6 fusion.27
  597.9 0.8 convolution_convert_fusion.3
  598.7 0.6 copy-done.3
  600.2 0.6 copy-done.31
  600.8 0.6 fusion.25
  601.7 0.6 convolution_convert_fusion.5
  602.3 0.6 convolution_convert_fusion.4
  602.9 7.7 fusion.69
  610.7 8.7 fusion.2
  619.5 1.2 copy-done.27
  620.6 8.7 fusion.103
  629.4 11.7 fusion.1
  641.2 1.6 copy-done.18
  642.8 9.2 fusion.78
  652.0 14.9 %fusion = bf16[4480,1120]{1,0:T(8,128)(2,1)} fusion(f32[4480,1120]{1,0:T(8,128)} %fusion.78, bf16[2,128,1120]{1,2,0:T(8,128)(2,1)S(1)} %copy-done.38, f32[128,4480]{1,0:T(8,128)} %fusion.105), kind=kOutput, calls=%fused_computation.3 | convolution fusion | flops 1299701760 | bytes 32686080 | tf_op jit(solution)/shard_map/dot_general | solution.py:33
  667.8 1.5 add_convert_fusion.3
  669.3 1.3 add_convert_fusion.2
  670.7 5.7 fusion.68
  676.4 3.7 fusion.66
  680.1 21.4 %all-reduce.13 = (bf16[1120]{0:T(1024)(128)(2,1)S(1)}, bf16[1120]{0:T(1024)(128)(2,1)S(1)}, bf16[1120]{0:T(1024)(128)(2,1)S(1)}, bf16[1120]{0:T(1024)(128)(2,1)S(1)}) all-reduce(bf16[1120]{0:T(1024)(128)(2,1)S(1)} %add_convert_fusion.5, ...), channel_id=2, replica_groups=mesh['wide'=8,'narrow'=4] {'narrow'}, use_global_device_ids=true, to_apply=%region_24.25.clone | all-reduce | flops 4480 | bytes 17920
  701.6 78.5 %reduce-scatter.13.cloned.1.call-done = bf16[280,3360]{1,0:T(8,128)(2,1)} async-done(((bf16[1120,3360]{1,0:T(8,128)(2,1)}), bf16[280,3360]{1,0:T(8,128)(2,1)}) %reduce-scatter.13.cloned.1.call-update) | async-done | bytes 1881616
  780.2 187.7 %reduce-scatter.17.cloned.1.call-done = bf16[280,4480]{1,0:T(8,128)(2,1)} async-done(((bf16[1120,4480]{1,0:T(8,128)(2,1)}), bf16[280,4480]{1,0:T(8,128)(2,1)}) %reduce-scatter.17.cloned.1.call-update) | async-done | bytes 2508816
  967.8 182.3 %reduce-scatter.11.cloned.1.call-done = bf16[1120,1120]{1,0:T(8,128)(2,1)} async-done(((bf16[4480,1120]{1,0:T(8,128)(2,1)}), bf16[1120,1120]{1,0:T(8,128)(2,1)}) %reduce-scatter.11.cloned.1.call-update) | async-done | bytes 2508816 | tf_op jit(solution)/shard_map/reduce_scatter | solution.py:231
  1150.3 14.7 %all-reduce.11 = (f32[280]{0:T(512)}, f32[280]{0:T(512)}, f32[280]{0:T(512)}, f32[280]{0:T(512)}) all-reduce(f32[280]{0:T(512)S(1)} %dynamic-slice_convert_fusion.3, f32[280]{0:T(512)S(1)} %dynamic-slice_convert_fusion.2, f32[280]{0:T(512)S(1)} %dynamic-slice_convert_fusion.1, ...), channel_id=1, replica_groups=mesh['wide'=8,'narrow'=4] {'wide'}, use_global_device_ids=true, to_apply=%region_25.26 | all-reduce | flops 1120 | bytes 8960 | tf_op jit(solution)/shard_map/psum | solution.py:237
  1165.1 8.3 fusion.6
  1173.6 8.4 fusion.7
  1182.0 0.9 pad_maximum_fusion.2
  1183.3 0.9 pad_maximum_fusion.3
  1184.2 90.5 %all-reduce.17.cloned.1.call-done = (bf16[280,3360]{1,0:T(8,128)(2,1)}, bf16[280,1120]{1,0:T(8,128)(2,1)}, bf16[280,4480]{1,0:T(8,128)(2,1)}, bf16[1120,1120]{1,0:T(8,128)(2,1)}) async-done(((bf16[280,3360]{1,0:T(8,128)(2,1)}, bf16[280,1120]{1,0:T(8,128)(2,1)}, bf16[280,4480]{1,0:T(8,128)(2,1)}, bf16[1120,1120]{1,0:T(8,128)(2,1)}), (bf16[280,3360]{1,0:T(8,128)(2,1)}, bf16[280,1120]{1,0:T(8,128)(2,1)}, ...) | async-done | bytes 7526416 | tf_op jit(solution)/shard_map/psum | solution.py:235
  1274.7 2.4 convert_element_type.225
  1277.1 2.2 convert_element_type.223
  1279.3 0.8 copy-done.36
  1280.0 2.6 convert_element_type.231
  1282.8 2.7 convert_element_type.233
  (238 shorter events, 10.8 us)
Async XLA Ops:
  7.2 144.3 %all-gather.5.cloned.1.call-start = ((), (), s32[]{:S(2)}) async-start(), calls=%async_computation.4 | async-start | bytes 9676800 | tf_op jit(solution)/shard_map/all_gather | solution.py:213
  7.9 197.4 %all-gather.7.cloned.1.call-start = ((), (), s32[]{:S(2)}) async-start(), calls=%async_computation.5 | async-start | bytes 3225600 | tf_op jit(solution)/shard_map/all_gather | solution.py:214
  8.7 2.9 copy-start.78
  8.7 3.2 copy-start.79
  8.7 3.4 copy-start.80
  8.7 24.8 %copy-start.76 = (s32[2]{0:T(128)S(1)}, s32[2]{0:T(128)}, u32[]{:S(2)}) copy-start(s32[2]{0:T(128)} %param.12) | copy-start | bytes 28
  8.7 26.7 %copy-start.12 = (bf16[2,128,1120]{1,2,0:T(8,128)(2,1)S(1)}, bf16[2,128,1120]{1,2,0:T(8,128)(2,1)}, u32[]{:S(2)}) copy-start(bf16[2,128,1120]{1,2,0:T(8,128)(2,1)} %param.11) | copy-start | bytes 1720324
  8.7 373.5 %all-gather.9.cloned.1.call-start = ((), (), s32[]{:S(2)}) async-start(), calls=%async_computation.6 | async-start | bytes 12544000 | tf_op jit(solution)/shard_map/all_gather | solution.py:217
  9.5 553.6 %all-gather.11.cloned.1.call-start = ((), (), s32[]{:S(2)}) async-start(), calls=%async_computation.7 | async-start | bytes 12902400 | tf_op jit(solution)/shard_map/all_gather | solution.py:218
  10.0 691.6 %reduce-scatter.15.cloned.1.call-start = ((), (), s32[]{:S(2)}) async-start(), calls=%async_computation.10 | async-start | bytes 3225600
  35.6 172.8 %copy-start.67 = (f32[128]{0:T(128)}, f32[128]{0:T(128)S(1)}, u32[]{:S(2)}) copy-start(f32[128]{0:T(128)S(1)} %get-tuple-element.80) | copy-start | bytes 1540
  35.6 567.3 %copy-start.60 = (f32[128]{0:T(128)}, f32[128]{0:T(128)S(1)}, u32[]{:S(2)}) copy-start(f32[128]{0:T(128)S(1)} %get-tuple-element.81) | copy-start | bytes 1540
  35.8 567.1 %copy-start.63 = (f32[128]{0:T(128)}, f32[128]{0:T(128)S(1)}, u32[]{:S(2)}) copy-start(f32[128]{0:T(128)S(1)} %add_rsqrt_fusion.3) | copy-start | bytes 1540
  35.8 172.6 %copy-start.71 = (f32[128]{0:T(128)}, f32[128]{0:T(128)S(1)}, u32[]{:S(2)}) copy-start(f32[128]{0:T(128)S(1)} %add_rsqrt_fusion.1) | copy-start | bytes 1540
  160.1 48.1 %copy-start.53 = (bf16[20,56,128]{2,1,0:T(8,128)(2,1)}, bf16[20,56,128]{2,1,0:T(8,128)(2,1)S(1)}, u32[]{:S(2)}) copy-start(bf16[20,56,128]{2,1,0:T(8,128)(2,1)S(1)} %convolution_convert_fusion.7) | copy-start | bytes 860164
  208.2 411.3 %copy-start.6 = (f32[128,1120]{0,1:T(8,128)}, f32[128,1120]{0,1:T(8,128)S(1)}, u32[]{:S(2)}) copy-start(f32[128,1120]{0,1:T(8,128)S(1)} %get-tuple-element.73) | copy-start | bytes 1720324
  216.5 3.8 copy-start.55
  563.1 9.2 copy-start
  576.9 8.2 copy-start.17
  576.9 8.2 copy-start.9
  577.0 8.2 copy-start.66
  585.1 3.9 copy-start.26
  593.3 186.8 %reduce-scatter.13.cloned.1.call-start = ((), (), s32[]{:S(2)}) async-start(), calls=%async_computation.9 | async-start | bytes 9676800
  597.5 13.2 %copy-start.40 = (bf16[20,56,128]{2,1,0:T(8,128)(2,1)}, bf16[20,56,128]{2,1,0:T(8,128)(2,1)S(1)}, u32[]{:S(2)}) copy-start(bf16[20,56,128]{2,1,0:T(8,128)(2,1)S(1)} %fusion.27) | copy-start | bytes 860164
  597.8 12.9 copy-start.41
  601.7 9.0 copy-start.44
  602.3 8.4 copy-start.46
  602.9 7.8 copy-start.48
  602.9 7.8 copy-start.68
  602.9 7.8 copy-start.72
  619.4 10.0 copy-start.10
  619.4 348.4 %reduce-scatter.17.cloned.1.call-start = ((), (), s32[]{:S(2)}) async-start(), calls=%async_computation.11 | async-start | bytes 12544000
  641.1 509.0 %reduce-scatter.11.cloned.1.call-start = ((), (), s32[]{:S(2)}) async-start(), calls=%async_computation.8 | async-start | bytes 12902400 | tf_op jit(solution)/shard_map/reduce_scatter | solution.py:231
  666.9 9.4 slice-start
  666.9 607.8 %all-reduce.17.cloned.1.call-start = ((), (), s32[]{:S(2)}) async-start(), calls=%async_computation.12 | async-start | bytes 15339520 | tf_op jit(solution)/shard_map/psum | solution.py:235
  670.6 5.7 slice-start.1
  670.6 5.7 copy-start.15
  670.6 5.8 copy-start.43
  670.6 5.8 copy-start.45
  670.6 5.8 copy-start.47
  670.6 5.8 copy-start.61
  670.6 5.8 copy-start.64
  670.6 5.8 copy-start.69
  670.7 5.8 copy-start.73
  676.4 3.7 copy-start.57
  1150.1 14.9 %copy-start.84 = (f32[128]{0:T(128)S(1)}, f32[128]{0:T(128)}, u32[]{:S(2)}) copy-start(f32[128]{0:T(128)} %get-tuple-element.17) | copy-start | bytes 1540
  1150.1 14.9 %copy-start.83 = (f32[128]{0:T(128)S(1)}, f32[128]{0:T(128)}, u32[]{:S(2)}) copy-start(f32[128]{0:T(128)} %get-tuple-element.18) | copy-start | bytes 1540
  1150.1 14.9 %copy-start.82 = (f32[128]{0:T(128)S(1)}, f32[128]{0:T(128)}, u32[]{:S(2)}) copy-start(f32[128]{0:T(128)} %get-tuple-element.20) | copy-start | bytes 1540
  1150.1 15.0 %copy-start.81 = (f32[128]{0:T(128)S(1)}, f32[128]{0:T(128)}, u32[]{:S(2)}) copy-start(f32[128]{0:T(128)} %get-tuple-element.21) | copy-start | bytes 1540
  1150.1 15.0 %copy-start.11 = (f32[128,1120]{0,1:T(8,128)S(1)}, f32[128,1120]{0,1:T(8,128)}, u32[]{:S(2)}) copy-start(f32[128,1120]{0,1:T(8,128)} %copy-done.8) | copy-start | bytes 1720324
  1150.1 15.0 %copy-start.20 = (f32[128,4480]{1,0:T(8,128)S(1)}, f32[128,4480]{1,0:T(8,128)}, u32[]{:S(2)}) copy-start(f32[128,4480]{1,0:T(8,128)} %fusion.105) | copy-start | bytes 6881284
  1165.1 8.4 copy-start.7
  1165.1 8.4 copy-start.19
  1173.5 9.4 copy-start.16
  1173.5 9.4 copy-start.23
  1173.5 9.4 copy-start.25
  1173.5 9.4 copy-start.58
  1173.5 9.4 copy-start.59
  1173.5 9.4 copy-start.62
  1173.6 9.4 copy-start.65
  1173.6 9.4 copy-start.70
  1173.6 9.4 copy-start.74
  1277.1 2.9 copy-start.36
  1280.0 2.8 copy-start.29
  (32 other events, 48.1 us)
Sparse Core Ops, SparseCore 0:
  9.6 141.9 all-gather.4
  153.1 52.2 all-gather.6
  206.9 175.2 all-gather.8
  383.7 179.3 all-gather.10
  593.5 49.2 reduce-scatter.14
  644.9 135.2 reduce-scatter.12
  782.5 185.2 reduce-scatter.16
  970.2 179.8 reduce-scatter.10
  1153.9 120.8 all-reduce.16

commit v2 on v1

v2 whole, which is shorter than its diff:
```python
import math

import jax
import jax.numpy as jnp
from jax import lax
from jax.experimental import pallas as pl
from jax.experimental.pallas import tpu as pltpu
from jax.sharding import PartitionSpec as P

HEADS = 20
EPS = 1e-05
MASKED = -1e30
BF, F32 = jnp.bfloat16, jnp.float32
MESH = pl.DeviceIdType.MESH

NZ = 4
NT = 4
WAVES = 2
SEQ = 128
NB = NT * WAVES
GELU_C = math.sqrt(2.0 / math.pi)
GELU_A = 0.044715


def up16(n):
    return -(-n // 16) * 16


def up128(n):
    return -(-n // 128) * 128


def nn(a, b):
    return lax.dot_general(a, b, (((1,), (0,)), ((), ())), preferred_element_type=F32)


def nt(a, b):
    return lax.dot_general(a, b, (((1,), (1,)), ((), ())), preferred_element_type=F32)


def tn(a, b):
    return lax.dot_general(a, b, (((0,), (0,)), ((), ())), preferred_element_type=F32)


def layer_kernel(
    dim, ff,
    tok_h, dy_h, wq_h, wo_h, wf_h, wp_h, len_s, lnv,
    res_o, gtok_o, gq_o, go_o, gf_o, gp_o, gln_o,
    tok, dys, xown, wq, wo, wf, wp, first, qs, ks, vs, pm, att, part, ra, sb, rb, mix, dmix,
    sec, act, gel, datt, dqkv, gq, go, gf, gp, yq, yo, yf, yp, zq, zo, zf, zp,
    lnr, vec, lens, lg, lr, lz,
    raw_sem, ag_sem, rs_sem, fin_sem, xs_sem, xa_sem, ln_sem,
):
    blk = dim // NZ
    bp = up16(blk)
    hb = bp // 2
    dp = NZ * bp
    nq = wq.shape[1]
    head = dim // HEADS
    nh = HEADS // NT
    inv_dim = 1.0 / dim
    scale = head ** (-0.5)

    w = lax.axis_index("wide")
    z = lax.axis_index("narrow")
    c = lax.rem(w, 2)
    x = lax.rem(w // 2, 2)
    y = lax.rem(w // 4, 2)
    t = 2 * x + c
    core_dev = (w + 1 - 2 * c, z)
    x_dev = (w + 2 - 4 * x, z)
    y_dev = (w + 4 - 8 * y, z)
    up_dev = (w, z + 1)
    down_dev = (w, z - 1)

    ends = []

    def remote(src, dst, ssem, rsem, dev):
        return pltpu.make_async_remote_copy(
            src_ref=src, dst_ref=dst, send_sem=ssem, recv_sem=rsem, device_id=dev, device_id_type=MESH
        )

    def send(make, cond=None, track=True):
        if cond is None:
            make().start()
        else:
            pl.when(cond())(lambda: make().start())
        if track:
            ends.append((cond, make))

    def both(a, b):
        return jnp.logical_and(a, b)

    lane = lax.broadcasted_iota(jnp.int32, (1, dp), 1)
    live = lax.rem(lane, bp) < blk
    livef = live.astype(F32)

    barrier = pltpu.get_barrier_semaphore()
    others = [(w, lax.rem(z + k, NZ)) for k in range(1, NZ)]
    for dev in [core_dev, x_dev, y_dev] + others:
        pl.semaphore_signal(barrier, inc=1, device_id=dev, device_id_type=MESH)
    pl.semaphore_wait(barrier, 3 + len(others))

    def rows_of(s, yy, r0=0, nr=None):
        return pl.ds(pl.multiple_of(bp * s + hb * yy + r0, 16), hb if nr is None else nr)

    q_pieces = [(0, 80), (80, hb - 80)]
    gathers = {
        "q": (wq, 0, q_pieces),
        "f": (wf, 4 * len(q_pieces), [(0, hb)]),
        "p": (wp, 4 * len(q_pieces) + 4, [(0, hb)]),
        "o": (wo, 4 * len(q_pieces) + 8, [(0, hb)]),
    }

    def ag_view(name, s, yy, piece):
        ref, base, pieces = gathers[name]
        r0, nr = pieces[piece]
        if name == "o":
            return ref.at[rows_of(0, yy, r0, nr)]
        return ref.at[rows_of(s, yy, r0, nr)]

    def ag_id(name, s, piece):
        ref, base, pieces = gathers[name]
        return base if name == "o" else base + 4 * piece + s

    def ag_z(name, s, piece, up):
        v = ag_view(name, s, y, piece)
        i = ag_id(name, s, piece)
        return remote(v, v, ag_sem.at[i, 0 if up else 1], ag_sem.at[i, 2], up_dev if up else down_dev)

    def ag_y(name, s, yy, piece):
        v = ag_view(name, s, yy, piece)
        i = ag_id(name, s, piece)
        return remote(v, v, ag_sem.at[i, 3], ag_sem.at[i, 4], y_dev)

    def ag_start(name):
        for piece in range(len(gathers[name][2])):
            def own():
                return (t == z) if name == "o" else (z >= 0)

            send(lambda p=piece: ag_z(name, z, p, True), lambda: both(own(), z < NZ - 1))
            send(lambda p=piece: ag_z(name, z, p, False), lambda: both(own(), z > 0))

    def ag_forward(name, k):
        for piece in range(len(gathers[name][2])):
            for up in (True, False):
                s = z - k if up else z + k
                ok = (z >= k) if up else (z + k <= NZ - 1)
                if name == "o":
                    ok = t == s
                more = (z < NZ - 1) if up else (z > 0)
                pl.when(ok)(lambda s=s, p=piece, u=up: ag_z(name, s, p, u).wait_recv())
                send(lambda s=s, p=piece, u=up: ag_z(name, s, p, u), lambda ok=ok, more=more: both(ok, more))
                send(lambda s=s, p=piece: ag_y(name, s, y, p), lambda ok=ok: ok)

    def ag_finish(name):
        for piece in range(len(gathers[name][2])):
            if name == "o":
                pl.when(z != t)(lambda p=piece: ag_y(name, 0, 1 - y, p).wait_recv())
            else:
                for s in range(NZ):
                    pl.when(z != s)(lambda s=s, p=piece: ag_y(name, s, 1 - y, p).wait_recv())

    def blk_of(s, cc, xx):
        return s * NT + cc * 2 + xx

    def xg(ref, e, s, kind):
        i = 2 * e + s
        if kind == "x":
            v = ref.at[blk_of(s, c, x)]
            return remote(v, v, xs_sem.at[i, 0], xs_sem.at[i, 1], x_dev)
        if kind == "own":
            v = ref.at[blk_of(s, c, x)]
            return remote(v, v, xs_sem.at[i, 2], xs_sem.at[i, 3], core_dev)
        v = ref.at[blk_of(s, c, 1 - x)]
        return remote(v, v, xs_sem.at[i, 4], xs_sem.at[i, 5], core_dev)

    def xg_start(ref, e, s, track=True):
        send(lambda: xg(ref, e, s, "x"), track=track)
        send(lambda: xg(ref, e, s, "own"), track=track)

    def xg_forward(ref, e, s, track=True):
        xg(ref, e, s, "x").wait_recv()
        send(lambda: xg(ref, e, s, "fwd"), track=track)

    def xg_finish(ref, e, s):
        xg(ref, e, s, "own").wait_recv()
        xg(ref, e, s, "fwd").wait_recv()

    def xg_sent(ref, e, s):
        for kind in ("x", "own", "fwd"):
            xg(ref, e, s, kind).wait_send()

    def ex_a(e, s):
        i = 2 * e + s
        return remote(
            part.at[pl.ds(s * NT + (1 - c) * 2, 2)], ra.at[int(e == 1), s],
            xa_sem.at[i, 0], xa_sem.at[i, 1], core_dev,
        )

    def ex_b(e, s):
        i = 2 * e + s
        return remote(sb.at[int(e == 1), s], rb.at[int(e == 1), s], xa_sem.at[i, 2], xa_sem.at[i, 3], x_dev)

    def ex_relay(e, s):
        ex_a(e, s).wait_recv()
        sb[int(e == 1), s] = (
            part[blk_of(s, c, 1 - x)].astype(F32) + ra[int(e == 1), s, 1 - x].astype(F32)
        ).astype(BF)
        ex_b(e, s).start()

    def ex_sum(e, s):
        ex_b(e, s).wait_recv()
        return (
            part[blk_of(s, c, x)].astype(F32)
            + ra[int(e == 1), s, x].astype(F32)
            + rb[int(e == 1), s].astype(F32)
        )

    def ex_sent(e):
        for s in range(WAVES):
            ex_a(e, s).wait_send()
            ex_b(e, s).wait_send()

    reduces = {"q": (gq, yq, zq, 0), "f": (gf, yf, zf, 1), "p": (gp, yp, zp, 2), "o": (go, yo, zo, 3)}

    def rs_y(name, d):
        g, yr, zr, i = reduces[name]
        if name == "o":
            return remote(g.at[rows_of(0, 1 - y)], yr.at[0], rs_sem.at[i, 0], rs_sem.at[i, 4], y_dev)
        return remote(g.at[rows_of(d, 1 - y)], yr.at[d], rs_sem.at[i, d], rs_sem.at[i, 4 + d], y_dev)

    def rs_z(name, d, slot, up):
        g, yr, zr, i = reduces[name]
        dd = 0 if name == "o" else d
        return remote(yr.at[dd], zr.at[slot], rs_sem.at[i, 8 + dd], rs_sem.at[i, 12 + slot], up_dev if up else down_dev)

    def add_up(dst, srcs):
        step = 48

        def body(j, carry):
            r = pl.ds(pl.multiple_of(j * step, step), step)
            total = srcs[0][r, :].astype(F32)
            for src in srcs[1:]:
                total = total + src[r, :].astype(F32)
            dst[r, :] = total.astype(BF)
            return carry

        lax.fori_loop(0, hb // step, body, 0)

    def rs_start(name, dests=(3, 0, 2, 1)):
        for d in (0,) if name == "o" else dests:
            send(lambda d=d: rs_y(name, d))

    def rs_stage(name, d, j):
        g, yr, zr, i = reduces[name]

        def side(pos, up):
            def run():
                rs_y(name, d).wait_recv()
                own = g.at[rows_of(0 if name == "o" else d, y)]
                mine = yr.at[0 if name == "o" else d]
                srcs = [own, mine]
                slot = 0 if name == "o" else d
                if j > 0:
                    rs_z(name, d, slot, up).wait_recv()
                    srcs.append(zr.at[slot])
                add_up(mine, srcs)

            nxt = pos + 1 if up else pos - 1
            if name == "o":
                last = t == nxt
                cond = both(z == pos, (t > pos) if up else (t < pos))
                pl.when(cond)(run)
                if up:
                    send(lambda: rs_z(name, 0, 1, True), lambda: both(cond, last))
                    send(lambda: rs_z(name, 0, 0, True), lambda: both(cond, jnp.logical_not(last)))
                else:
                    send(lambda: rs_z(name, 0, 0, False), lambda: cond)
            else:
                cond = z == pos
                pl.when(cond)(run)
                slot = NZ if (up and nxt == d) else d
                send(lambda: rs_z(name, d, slot, up), lambda: cond)

        if name == "o":
            if j < NZ - 1:
                side(j, True)
                side(NZ - 1 - j, False)
            return
        if j < d:
            side(j, True)
        if NZ - 1 - j > d:
            side(NZ - 1 - j, False)

    def rs_final(name):
        g, yr, zr, i = reduces[name]
        out = name == "o"
        me = 0 if out else z
        here = (t == z) if out else (z >= 0)
        above = 0 if out else z
        below = 1 if out else NZ

        def run(has_above, has_below):
            def go_():
                rs_y(name, me).wait_recv()
                srcs = [g.at[rows_of(me, y)], yr.at[me]]
                if has_above:
                    rs_z(name, me, above, True).wait_recv()
                    srcs.append(zr.at[above])
                if has_below:
                    rs_z(name, me, below, True).wait_recv()
                    srcs.append(zr.at[below])
                add_up(yr.at[me], srcs)
            return go_

        pl.when(both(here, z == 0))(run(True, False))
        pl.when(both(here, z == NZ - 1))(run(False, True))
        pl.when(both(here, both(z > 0, z < NZ - 1)))(run(True, True))

    outs = {"q": gq_o, "f": gf_o, "p": gp_o, "o": go_o}

    def fin_view(name, tt, yy):
        return outs[name].at[yy] if name == "o" else outs[name].at[tt * 2 + yy]

    def fin_copy(name, src, tt, yy, k, dev):
        i = reduces[name][3]
        slot = yy if name == "o" else tt * 2 + yy
        return remote(src, fin_view(name, tt, yy), fin_sem.at[i, k], fin_sem.at[i, 8 + slot], dev)

    def own_block(name):
        yr = reduces[name][1]
        return yr.at[0] if name == "o" else yr.at[z]

    def keep_own(name):
        return pltpu.make_async_copy(own_block(name), fin_view(name, t, y), fin_sem.at[reduces[name][3], 7])

    tx = 2 * (1 - x) + c

    def fin_start(name):
        here = (lambda: t == z) if name == "o" else None
        if here is None:
            keep_own(name).start()
        else:
            pl.when(here())(lambda: keep_own(name).start())
        send(lambda: fin_copy(name, own_block(name), t, y, 0, y_dev), here)
        send(lambda: fin_copy(name, own_block(name), t, y, 1, x_dev), here)
        send(lambda: fin_copy(name, own_block(name), t, y, 2, core_dev), here)

    def fin_wait(name, tt, yy):
        fin_copy(name, fin_view(name, tt, yy), tt, yy, 0, core_dev).wait_recv()

    def fin_forward_y(name):
        here = (t == z) if name == "o" else (z >= 0)
        pl.when(here)(lambda: fin_wait(name, t, 1 - y))
        v = fin_view(name, t, 1 - y)
        send(lambda: fin_copy(name, v, t, 1 - y, 3, x_dev), lambda: here)
        send(lambda: fin_copy(name, v, t, 1 - y, 4, core_dev), lambda: here)

    def fin_forward_x(name):
        here = (tx == z) if name == "o" else (z >= 0)
        for k, yy in ((5, y), (6, 1 - y)):
            pl.when(here)(lambda yy=yy: fin_wait(name, tx, yy))
            send(lambda k=k, yy=yy: fin_copy(name, fin_view(name, tx, yy), tx, yy, k, core_dev), lambda: here)

    def fin_finish(name):
        if name == "o":
            here = lax.rem(z, 2) != c
            for yy in range(2):
                pl.when(here)(lambda yy=yy: fin_wait(name, 0, yy))
            pl.when(t == z)(lambda: keep_own(name).wait())
        else:
            for xx in range(2):
                for yy in range(2):
                    fin_wait(name, 2 * xx + (1 - c), yy)
            keep_own(name).wait()

    base = pl.multiple_of(bp * z, 16)

    def prepare(rq, rt, ro, rd):
        loads = [
            pltpu.make_async_copy(wq_h, rq, raw_sem.at[0]),
            pltpu.make_async_copy(tok_h, rt, raw_sem.at[1]),
            pltpu.make_async_copy(wo_h, ro, raw_sem.at[2]),
            pltpu.make_async_copy(dy_h, rd, raw_sem.at[3]),
        ]
        for load in loads:
            load.start()
        lnr[z] = lnv[...]
        for k in range(1, NZ):
            send(lambda k=k: remote(lnv, lnr.at[z], ln_sem.at[k - 1], ln_sem.at[2 + k], others[k - 1]))

        loads[0].wait()
        wq[pl.ds(base, bp), :] = jnp.zeros((bp, nq), BF)
        for k in range(NT):
            @pl.when(t == k)
            def _(k=k):
                for j in range(3):
                    wq[pl.ds(base, blk), blk * j : blk * (j + 1)] = rq[:, dim * j + blk * k : dim * j + blk * (k + 1)]
        ag_start("q")

        def spread(dst, src):
            dst[...] = jnp.zeros((SEQ, dp), BF)
            for j in range(NZ):
                dst[:, bp * j : bp * j + blk] = src[:, blk * j : blk * (j + 1)]

        loads[1].wait()
        for s in range(WAVES):
            spread(xown.at[s], rt.at[pl.ds(SEQ * s, SEQ)])
            sent = jnp.where(lane == blk, len_s[s].astype(F32), xown[s].astype(F32))
            tok[blk_of(s, c, x)] = sent.astype(BF)
            xg_start(tok, 0, s, track=False)
        loads[2].wait()

        @pl.when(t == z)
        def _():
            wo[...] = jnp.zeros_like(wo)
            for j in range(NZ):
                wo[0:blk, bp * j : bp * j + blk] = ro[:, blk * j : blk * (j + 1)]
        ag_start("o")
        loads[3].wait()
        for s in range(WAVES):
            spread(dys.at[blk_of(s, c, x)], rd.at[pl.ds(SEQ * s, SEQ)])
            xg_start(dys, 1, s)

    def prepare_mlp(rf, rp):
        loads = [
            pltpu.make_async_copy(wf_h, rf, raw_sem.at[4]),
            pltpu.make_async_copy(wp_h.at[pl.ds(pl.multiple_of(blk * t, 8), blk)], rp, raw_sem.at[5]),
        ]
        for load in loads:
            load.start()
        loads[0].wait()
        wf[pl.ds(base, bp), :] = jnp.zeros((bp, dp), BF)
        for k in range(NT):
            @pl.when(t == k)
            def _(k=k):
                for j in range(NZ):
                    lo = (ff // NZ) * j + blk * k
                    wf[pl.ds(base, blk), bp * j : bp * j + blk] = rf[:, lo : lo + blk]
        loads[1].wait()
        wp[pl.ds(base, bp), :] = jnp.zeros((bp, dp), BF)
        for j in range(NZ):
            wp[pl.ds(base, blk), bp * j : bp * j + blk] = rp[:, blk * j : blk * (j + 1)]

    pl.run_scoped(
        prepare,
        pltpu.VMEM((blk, 3 * dim), BF),
        pltpu.VMEM((WAVES * SEQ, dim), BF),
        pltpu.VMEM((blk, dim), BF),
        pltpu.VMEM((WAVES * SEQ, dim), BF),
    )
    pl.run_scoped(prepare_mlp, pltpu.VMEM((blk, ff), BF), pltpu.VMEM((blk, dim), BF))

    for k in range(1, NZ):
        remote(lnv, lnr.at[lax.rem(z + NZ - k, NZ)], ln_sem.at[k - 1], ln_sem.at[2 + k], others[k - 1]).wait_recv()
    vec[...] = jnp.zeros_like(vec)
    for j in range(NZ):
        vec[:, bp * j : bp * j + blk] = lnr[j, :, 0:blk]
    lg[...] = jnp.zeros_like(lg)
    dqkv[...] = jnp.zeros_like(dqkv)

    def stats(rows):
        mean = jnp.sum(rows, axis=-1, keepdims=True) * inv_dim
        cen = (rows - mean) * livef
        inv = lax.rsqrt(jnp.sum(cen * cen, axis=-1, keepdims=True) * inv_dim + EPS)
        return cen * inv, inv

    def norm_back(e, n, inv):
        me = jnp.sum(e, axis=-1, keepdims=True) * inv_dim
        mn = jnp.sum(e * n, axis=-1, keepdims=True) * inv_dim
        return inv * (e - me - n * mn) * livef

    def ln_first(s):
        def body(i, carry):
            b = s * NT + i
            raw = tok[b].astype(F32)
            lens[b] = jnp.broadcast_to(raw[0:8, blk : blk + 1], (8, SEQ))
            n, inv = stats(raw * livef)
            first[b] = (n * vec[0:1, :] + vec[1:2, :]).astype(BF)
            return carry
        lax.fori_loop(0, NT, body, 0)

    lane_h = lax.broadcasted_iota(jnp.int32, (1, bp), 1)
    head_masks = [(lane_h >= head * h) & (lane_h < head * (h + 1)) for h in range(nh)]

    def stack_heads(v):
        zero = jnp.zeros_like(v)
        return jnp.concatenate([jnp.where(m, v, zero) for m in head_masks], axis=0)

    def side_by_side(v):
        return jnp.concatenate([v[SEQ * h : SEQ * (h + 1)] for h in range(nh)], axis=1)

    def project(s):
        def body(i, carry):
            b = s * NT + i * 2
            rows = first[pl.ds(b, 2)].reshape(2 * SEQ, dp)
            out = nn(rows, wq[...])
            for j, ref in enumerate((qs, ks, vs)):
                ref[pl.ds(b, 2)] = out[:, blk * j : blk * j + bp].astype(BF).reshape(2, SEQ, bp)
            return carry
        lax.fori_loop(0, 2, body, 0)

    def attend(s):
        q_pos = lax.broadcasted_iota(jnp.int32, (SEQ, SEQ), 0)
        k_pos = lax.broadcasted_iota(jnp.int32, (SEQ, SEQ), 1)

        def body(i, carry):
            b = s * NT + i
            scores = nt(stack_heads(qs[b]), ks[b]) * scale
            ok = (k_pos <= q_pos) & (k_pos.astype(F32) < lens[b, 0:1, :])
            bias = jnp.concatenate([ok.astype(F32)] * nh, axis=0) > 0.5
            scores = jnp.where(bias, scores, MASKED)
            top = jnp.max(scores, axis=-1, keepdims=True)
            ex = jnp.exp(scores - top)
            prob = ex / jnp.sum(ex, axis=-1, keepdims=True)
            pm[b] = prob
            out = nn(side_by_side(prob.astype(BF)), stack_heads(vs[b]))
            att[b] = out.astype(BF)
            return carry
        lax.fori_loop(0, NT, body, 0)

    def matmul_part(src, weight, s, transposed):
        width = src.shape[2]

        def body(i, carry):
            b = s * NT + i * 2
            rows = src[pl.ds(b, 2)].reshape(2 * SEQ, width)
            out = nt(rows, weight[...]) if transposed else nn(rows, weight[...])
            part[pl.ds(b, 2)] = out.astype(BF).reshape(2, SEQ, dp)
            return carry
        lax.fori_loop(0, 2, body, 0)

    ag_forward("q", 1)
    xg_forward(tok, 0, 0, track=False)
    ag_forward("q", 2)
    ag_start("f")
    ag_forward("o", 1)
    xg_finish(tok, 0, 0)
    ln_first(0)
    xg_forward(tok, 0, 1, track=False)
    ag_forward("q", 3)
    xg_finish(tok, 0, 1)
    ln_first(1)
    ag_forward("o", 2)
    ag_start("p")
    ag_forward("f", 1)
    ag_forward("o", 3)
    ag_finish("q")
    project(0)
    attend(0)
    ag_finish("o")
    matmul_part(att, wo, 0, False)
    ex_a(0, 0).start()
    ag_forward("f", 2)
    project(1)
    attend(1)
    matmul_part(att, wo, 1, False)
    ex_a(0, 1).start()
    ex_relay(0, 0)
    ag_forward("f", 3)
    ag_forward("p", 1)
    ex_relay(0, 1)
    xg_forward(dys, 1, 0)
    xg_forward(dys, 1, 1)

    def mid(s):
        rows = xown[s].astype(F32) + ex_sum(0, s)
        mix[s] = rows
        n, inv = stats(rows)
        sec[blk_of(s, c, x)] = (n * vec[2:3, :] + vec[3:4, :]).astype(BF)
        xg_start(sec, 2, s)

    mid(0)
    mid(1)
    ag_forward("p", 2)
    xg_forward(sec, 2, 0)
    xg_forward(sec, 2, 1)
    ag_forward("p", 3)
    for s in range(WAVES):
        xg_sent(tok, 0, s)
    ex_sent(0)
    ag_finish("f")

    def expand(s):
        def body(i, carry):
            b = s * NT + i * 2
            rows = sec[pl.ds(b, 2)].reshape(2 * SEQ, dp)
            pre = nn(rows, wf[...])
            sq = pre * pre
            th = jnp.tanh(GELU_C * (pre + GELU_A * (pre * sq)))
            half = 0.5 * (1.0 + th)
            act[pl.ds(b, 2)] = (pre * half).astype(BF).reshape(2, SEQ, dp)
            slope = half + (0.5 * GELU_C) * pre * (1.0 - th * th) * (1.0 + (3.0 * GELU_A) * sq)
            gel[pl.ds(b, 2)] = slope.astype(BF).reshape(2, SEQ, dp)
            return carry
        lax.fori_loop(0, 2, body, 0)

    for s in range(WAVES):
        xg_finish(sec, 2, s)
        expand(s)
    for s in range(WAVES):
        xg_finish(dys, 1, s)

    def grad_of(dst, left, right):
        step = 384
        rows = NB * SEQ

        def body(j, carry):
            cols = pl.ds(pl.multiple_of(j * step, step), step)
            out = tn(left[:, :, cols].reshape(rows, step), right[...].reshape(rows, right.shape[2]))
            dst[cols, :] = out.astype(BF)
            return carry
        lax.fori_loop(0, dp // step, body, 0)

    grad_of(gp, act, dys)
    rs_start("p")
    ag_finish("p")

    def back_act(s):
        def body(i, carry):
            b = s * NT + i * 2
            d_act = nt(dys[pl.ds(b, 2)].reshape(2 * SEQ, dp), wp[...])
            slope = gel[pl.ds(b, 2)].reshape(2 * SEQ, dp).astype(F32)
            gel[pl.ds(b, 2)] = (d_act * slope).astype(BF).reshape(2, SEQ, dp)
            return carry
        lax.fori_loop(0, 2, body, 0)

    for s in range(WAVES):
        back_act(s)
        matmul_part(gel, wf, s, True)
        ex_a(2, s).start()
    rs_stage("p", 3, 0)
    rs_stage("p", 0, 0)
    ex_relay(2, 0)
    ex_relay(2, 1)
    grad_of(gf, sec, gel)
    rs_start("f")
    for d in (2, 1):
        rs_stage("p", d, 0)
    for d in (3, 0):
        rs_stage("p", d, 1)

    def back_mid(s):
        d2 = ex_sum(2, s)
        n, inv = stats(mix[s])
        lg[2:3, :] = lg[2:3, :] + jnp.sum(d2 * n, axis=0, keepdims=True)
        lg[3:4, :] = lg[3:4, :] + jnp.sum(d2, axis=0, keepdims=True)
        rows = dys[blk_of(s, c, x)].astype(F32) + norm_back(d2 * vec[2:3, :], n, inv)
        dmix[s] = rows
        tok[blk_of(s, c, x)] = rows.astype(BF)
        xg_start(tok, 3, s)

    back_mid(0)
    back_mid(1)
    ex_sent(2)
    for d in (2, 1):
        rs_stage("p", d, 1)
    for d in (3, 0):
        rs_stage("p", d, 2)
    for s in range(WAVES):
        matmul_part(act, wp, s, False)
        ex_a(1, s).start()
    xg_forward(tok, 3, 0)
    xg_forward(tok, 3, 1)
    ex_relay(1, 0)
    ex_relay(1, 1)
    rs_final("p")
    fin_start("p")

    def back_attend(s):
        def proj(i, carry):
            b = s * NT + i * 2
            out = nt(tok[pl.ds(b, 2)].reshape(2 * SEQ, dp), wo[...])
            datt[pl.ds(b, 2)] = out.astype(BF).reshape(2, SEQ, bp)
            return carry
        lax.fori_loop(0, 2, proj, 0)

        def body(i, carry):
            b = s * NT + i
            d_out = stack_heads(datt[b])
            prob = pm[b]
            d_prob = nt(d_out, vs[b])
            total = jnp.sum(prob * d_prob, axis=-1, keepdims=True)
            d_scores = (prob * (d_prob - total)).astype(BF)
            dqkv[b, :, 0:bp] = (nn(side_by_side(d_scores), stack_heads(ks[b])) * scale).astype(BF)
            dqkv[b, :, blk : blk + bp] = (tn(d_scores, stack_heads(qs[b])) * scale).astype(BF)
            dqkv[b, :, 2 * blk : 2 * blk + bp] = tn(prob.astype(BF), d_out).astype(BF)
            return carry
        lax.fori_loop(0, NT, body, 0)

    xg_finish(tok, 3, 0)
    back_attend(0)
    for d in (3, 0, 2, 1):
        rs_stage("f", d, 0)
    xg_finish(tok, 3, 1)
    back_attend(1)
    rows_all = NB * SEQ
    go[...] = tn(att[...].reshape(rows_all, bp), tok[...].reshape(rows_all, dp)).astype(BF)
    rs_start("o")
    grad_of(gq, first, dqkv)
    rs_start("q")
    for d in (3, 0, 2, 1):
        rs_stage("f", d, 1)

    for s in range(WAVES):
        rows = (mix[s] + ex_sum(1, s)).astype(BF)
        for j in range(NZ):
            res_o[SEQ * s : SEQ * (s + 1), blk * j : blk * (j + 1)] = rows[:, bp * j : bp * j + blk]
    ex_sent(1)
    for s in range(WAVES):
        matmul_part(dqkv, wq, s, True)
        ex_a(3, s).start()
    for d in (3, 0):
        rs_stage("f", d, 2)
    ex_relay(3, 0)
    ex_relay(3, 1)
    rs_final("f")
    fin_start("f")
    fin_forward_y("p")
    rs_stage("o", 0, 0)
    fin_forward_x("p")
    rs_stage("o", 0, 1)
    for d in (3, 0, 2, 1):
        rs_stage("q", d, 0)

    def back_first(s):
        d1 = ex_sum(3, s)
        n, inv = stats(xown[s].astype(F32))
        lg[0:1, :] = lg[0:1, :] + jnp.sum(d1 * n, axis=0, keepdims=True)
        lg[1:2, :] = lg[1:2, :] + jnp.sum(d1, axis=0, keepdims=True)
        rows = (dmix[s] + norm_back(d1 * vec[0:1, :], n, inv)).astype(BF)
        for j in range(NZ):
            gtok_o[SEQ * s : SEQ * (s + 1), blk * j : blk * (j + 1)] = rows[:, bp * j : bp * j + blk]

    back_first(0)
    back_first(1)
    ex_sent(3)
    rs_stage("o", 0, 2)
    for d in (3, 0, 2, 1):
        rs_stage("q", d, 1)
    rs_final("o")
    fin_start("o")
    fin_forward_y("f")
    fin_forward_x("f")

    for k, dev in enumerate((core_dev, x_dev, y_dev)):
        hop = remote(lg, lr.at[k], ln_sem.at[6 + 2 * k], ln_sem.at[7 + 2 * k], dev)
        hop.start()
        hop.wait()
        lg[...] = lg[...] + lr[k]
    for k in range(1, NZ):
        send(lambda k=k: remote(lg, lz.at[k - 1], ln_sem.at[11 + k], ln_sem.at[14 + k], others[k - 1]))
    for d in (3, 0):
        rs_stage("q", d, 2)
    rs_final("q")
    fin_start("q")
    fin_forward_y("o")
    for k in range(1, NZ):
        remote(lg, lz.at[k - 1], ln_sem.at[11 + k], ln_sem.at[14 + k], others[k - 1]).wait_recv()
    total = lg[...] + lz[0] + lz[1] + lz[2]
    for j in range(NZ):
        @pl.when(z == j)
        def _(j=j):
            gln_o[:, 0:blk] = total[:, bp * j : bp * j + blk]
    fin_forward_x("o")
    fin_forward_y("q")
    fin_forward_x("q")
    for name in ("p", "f", "o", "q"):
        fin_finish(name)
    for cond, make in ends:
        if cond is None:
            make().wait_send()
        else:
            pl.when(cond())(lambda make=make: make().wait_send())


def layer_call(dim, ff, tokens, cot, w_qkv, w_out, w_fc, w_proj, lengths, lnv):
    blk = dim // NZ
    bp = up16(blk)
    hb = bp // 2
    dp = NZ * bp
    nq = up128(3 * blk)
    rows = WAVES * SEQ
    vm, dma = pltpu.VMEM, pltpu.SemaphoreType.DMA
    big = (NB, SEQ, dp)
    scratch = [
        vm(big, BF), vm(big, BF), vm((WAVES, SEQ, dp), BF),
        vm((dp, nq), BF), vm((bp, dp), BF), vm((dp, dp), BF), vm((dp, dp), BF),
        vm(big, BF),
        vm((NB, SEQ, bp), BF), vm((NB, SEQ, bp), BF), vm((NB, SEQ, bp), BF),
        vm((NB, (HEADS // NT) * SEQ, SEQ), F32),
        vm((NB, SEQ, bp), BF),
        vm(big, BF),
        vm((2, WAVES, 2, SEQ, dp), BF), vm((2, WAVES, SEQ, dp), BF), vm((2, WAVES, SEQ, dp), BF),
        vm((WAVES, SEQ, dp), F32), vm((WAVES, SEQ, dp), F32),
        vm(big, BF), vm(big, BF), vm(big, BF),
        vm((NB, SEQ, bp), BF), vm((NB, SEQ, nq), BF),
        vm((dp, nq), BF), vm((bp, dp), BF), vm((dp, dp), BF), vm((dp, dp), BF),
        vm((NZ, hb, nq), BF), vm((1, hb, dp), BF), vm((NZ, hb, dp), BF), vm((NZ, hb, dp), BF),
        vm((NZ + 1, hb, nq), BF), vm((2, hb, dp), BF), vm((NZ + 1, hb, dp), BF), vm((NZ + 1, hb, dp), BF),
        vm((NZ, 8, up128(blk)), F32), vm((8, dp), F32), vm((NB, 8, SEQ), F32),
        vm((8, dp), F32), vm((3, 8, dp), F32), vm((3, 8, dp), F32),
        dma((6,)), dma((17, 5)), dma((4, 17)), dma((4, 16)), dma((8, 6)), dma((8, 4)), dma((18,)),
    ]
    hbm = pl.BlockSpec(memory_space=pl.ANY)
    inv = pl.BlockSpec(memory_space=pltpu.VMEM)
    shape = jax.ShapeDtypeStruct

    def body(*refs):
        layer_kernel(dim, ff, *refs)

    return pl.pallas_call(
        body,
        out_shape=(
            shape((rows, dim), BF), shape((rows, dim), BF),
            shape((8, hb, nq), BF), shape((2, hb, dp), BF), shape((8, hb, dp), BF), shape((8, hb, dp), BF),
            shape((8, up128(blk)), F32),
        ),
        in_specs=[hbm] * 6 + [pl.BlockSpec(memory_space=pltpu.SMEM), inv],
        out_specs=(inv, inv, hbm, hbm, hbm, hbm, inv),
        scratch_shapes=scratch,
        compiler_params=pltpu.CompilerParams(
            collective_id=0, has_side_effects=True, vmem_limit_bytes=67043328
        ),
    )(tokens, cot, w_qkv, w_out, w_fc, w_proj, lengths, lnv)


def sum_boxes(value, wide):
    total = value
    for k in range(1, wide // 8):
        total = total + lax.ppermute(value, "wide", [(i, (i + 8 * k) % wide) for i in range(wide)])
    return total


def solution(mesh):
    wide, narrow = mesh.shape["wide"], mesh.shape["narrow"]
    assert narrow == NZ and wide % 8 == 0

    def shards(tokens, lengths, ln1_gain, ln1_bias, w_qkv, w_out, ln2_gain, ln2_bias, w_fc, w_proj, cotangent):
        cells, seq, dim = tokens.shape
        assert cells == WAVES and seq == SEQ
        ff = w_fc.shape[1]
        blk = dim // NZ
        bp = up16(blk)
        lnv = jnp.pad(
            jnp.stack([ln1_gain, ln1_bias, ln2_gain, ln2_bias]).astype(F32), ((0, 4), (0, up128(blk) - blk))
        )
        res, gtok, gq, go, gf, gp, gln = layer_call(
            dim, ff, tokens.reshape(cells * seq, dim), cotangent.reshape(cells * seq, dim),
            w_qkv, w_out, w_fc, w_proj, lengths, lnv,
        )
        gq = gq.reshape(NT, bp, gq.shape[2])[:, :blk, : 3 * blk].astype(F32)
        gq = gq.reshape(NT, blk, 3, blk).transpose(1, 2, 0, 3).reshape(blk, 3 * dim)
        go = go.reshape(bp, NZ, bp)[:blk, :, :blk].astype(F32).reshape(blk, dim)
        gf = gf.reshape(NT, bp, NZ, bp)[:, :blk, :, :blk].astype(F32)
        gf = gf.transpose(1, 2, 0, 3).reshape(blk, ff)
        gp = gp.reshape(NT, bp, NZ, bp)[:, :blk, :, :blk].astype(F32).reshape(NT * blk, dim)
        grads = [sum_boxes(g, wide) for g in (gq, go, gf, gp, gln)]
        gq, go, gf, gp, gln = grads
        return (
            res.reshape(cells, seq, dim), gtok.reshape(cells, seq, dim),
            gln[0, :blk], gln[1, :blk], gq, go, gln[2, :blk], gln[3, :blk], gf, gp,
        )

    rows = P(("wide", "narrow"), None, None)
    vec, mat = P("narrow"), P("narrow", None)
    return jax.shard_map(
        shards,
        mesh=mesh,
        in_specs=(rows, P(("wide", "narrow")), vec, vec, mat, mat, vec, vec, mat, mat, rows),
        out_specs=(rows, rows, vec, vec, mat, mat, vec, vec, mat, mat),
        check_vma=False,
    )
```

time: 1300 us -> 345 us (0.27)
  waiting for transfers between devices: 1040 us -> 0 us
  Pallas kernels: 0 us -> 261 us
  matrix products: 148 us -> 0 us
  blocking collectives: 57.2 us -> 0 us
  local copies, waits for them, and re-layouts: 13.7 us -> 70.6 us
  between operations: 17 us -> 0.94 us
    all_gather x4 -> x0, waiting for transfers between devices: 495 us -> none  [the longest x1 173 us: shards(): lax.all_gather(w_proj, 'narrow', axis=0, tiled=True)]
    unnamed x12 -> x0, waiting for transfers between devices: 269 us -> none
    pallas_call x0 -> x1, Pallas kernels: none -> 261 us  [layer_call(): pl.pallas_call(body, out_shape=(shape((rows, dim), BF), shape((rows, dim)...]
    reduce_scatter x1 -> x0, waiting for transfers between devices: 182 us -> none  [shards(): lax.psum_scatter(grad.astype(jnp.bfloat16), 'narrow', scatter_dimension=0...]
    dot_general x36 -> x0, matrix products: 148 us -> none  [the longest x8 64.1 us: inner_rows(): lax.dot_general(left, right, (((0,), (0,)), ((), ())), preferred_element_...]
    psum x1 -> x0, waiting for transfers between devices: 90.5 us -> none  [shards(): part = lax.psum(part, 'wide').astype(jnp.float32)]
    reshape x0 -> x9, local copies, waits for them, and re-layouts: none -> 54.4 us  [the longest x2 16.2 us: shards(): gf = gf.transpose(1, 2, 0, 3).reshape(blk, ff)]
    unnamed x2 -> x0, blocking collectives: 42.5 us -> none
  transfers between devices with their start and end apart: 9 -> 0, of which waited for: 8 -> 0; matrix products, arithmetic and copies ran while one was open for 10% -> 0% of each run, Pallas kernels for 0% -> 0%
where the time goes in v2:
time: 345 us; the launch traced here: 340 us
  Pallas kernels  261 us (76%)
  local copies, waits for them, and re-layouts  70.6 us (20%)
  other arithmetic  8.08 us (2%)
    pallas_call x1, Pallas kernels, layer_call(): pl.pallas_call(body, out_shape=(shape((rows, dim), BF), shape((rows, dim)...  261 us
    reshape x2, local copies, waits for them, and re-layouts, shards(): gf = gf.transpose(1, 2, 0, 3).reshape(blk, ff)  16.2 us
    reshape x2, local copies, waits for them, and re-layouts, shards(): gp.reshape(NT, bp, NZ, bp)[:, :blk, :, :blk].astype(F32)  14.7 us
    reshape x2, local copies, waits for them, and re-layouts, shards(): gq = gq.reshape(NT, blk, 3, blk).transpose(1, 2, 0, 3).reshape(blk, 3 * dim)  14.3 us
    unnamed x11, local copies, waits for them, and re-layouts  10.5 us

profile of v2, /device:TPU:0, one launch (start us, length us, event | category | flops | bytes accessed | tf_op | source)
XLA Modules:
  0.0 340.3 jit_solution(11442963370363713728)
XLA Ops:
  0.6 2.1 copy.33
  2.8 2.1 copy.34
  4.9 0.7 stack.15
  5.6 0.7 stack.16
  6.2 0.7 stack.17
  6.9 0.7 stack.18
  7.6 0.6 fusion.9.refs_7_
  8.2 260.7 %shard_map.186 = (bf16[256,1120]{1,0:T(8,128)(2,1)}, bf16[256,1120]{1,0:T(8,128)(2,1)}, bf16[8,144,896]{2,1,0:T(8,128)(2,1)}, bf16[2,144,1152]{2,1,0:T(8,128)(2,...) custom-call(bf16[256,1120]{1,0:T(8,128)(2,1)} %bitcast.12, ...), custom_call_target="tpu_custom_call" | custom-call | tf_op jit(solution)/shard_map/pallas_call | solution.py:813
  268.9 1.5 slice_reduce_fusion
  270.4 6.6 %reshape.83 = bf16[4,288,4,288]{3,2,1,0:T(4,128)(2,1)S(1)} reshape(bf16[8,144,1152]{2,1,0:T(8,128)(2,1)} %get-tuple-element.22) | data formatting | bytes 5308416 | tf_op jit(solution)/shard_map/reshape | solution.py:856
  277.0 0.9 convert_bitcast_fusion
  277.9 7.2 %copy.37 = f32[280,4,4,280]{3,2,1,0:T(4,128)} copy(f32[280,4,4,280]{3,1,0,2:T(4,128)S(1)} %convert_bitcast_fusion) | data formatting | bytes 10035200 | tf_op jit(solution)/shard_map/reshape | solution.py:857
  285.1 0.0 copy-start
  285.1 8.9 %reshape.94 = f32[280,4480]{1,0:T(8,128)} reshape(f32[280,4,4,280]{3,2,1,0:T(4,128)} %copy.37) | data formatting | bytes 10035200 | tf_op jit(solution)/shard_map/reshape | solution.py:857
  294.0 0.0 copy-done
  294.0 1.4 slice.32
  295.5 3.1 copy.40
  298.6 2.7 convert_bitcast_fusion.1
  301.3 8.3 %copy.36 = f32[280,3,4,280]{3,2,1,0:T(4,128)} copy(f32[280,3,4,280]{0,3,1,2:T(8,128)} %convert_bitcast_fusion.1) | data formatting | bytes 7526400 | tf_op jit(solution)/shard_map/reshape | solution.py:854
  309.6 6.0 %reshape.90 = f32[280,3360]{1,0:T(8,128)} reshape(f32[280,3,4,280]{3,2,1,0:T(4,128)} %copy.36) | data formatting | bytes 7526400 | tf_op jit(solution)/shard_map/reshape | solution.py:854
  315.6 6.7 %reshape.86 = bf16[4,288,4,288]{3,2,1,0:T(4,128)(2,1)S(1)} reshape(bf16[8,144,1152]{2,1,0:T(8,128)(2,1)} %get-tuple-element.23) | data formatting | bytes 5308416 | tf_op jit(solution)/shard_map/reshape | solution.py:858
  322.3 3.7 %slice_convert_fusion = f32[4,280,4,280]{3,2,1,0:T(4,128)} fusion(bf16[4,288,4,288]{3,2,1,0:T(4,128)(2,1)S(1)} %reshape.86), kind=kLoop, calls=%fused_computation.2 | loop fusion | flops 1254400 | bytes 7526400 | tf_op jit(solution)/shard_map/reshape | solution.py:858
  326.0 0.0 copy-start.1
  326.0 8.0 %reshape.96 = f32[1120,1120]{1,0:T(8,128)} reshape(f32[4,280,4,280]{3,2,1,0:T(4,128)} %slice_convert_fusion) | data formatting | bytes 10035200 | tf_op jit(solution)/shard_map/reshape | solution.py:858
  334.0 0.0 copy-done.1
  334.0 0.8 reshape.80
  334.8 0.0 copy-start.2
  334.8 0.2 slice_convert_fusion.1
  335.0 1.9 reshape.92
  336.9 2.1 copy.38
  339.0 0.0 copy-done.2
  339.0 1.1 copy.39
Async XLA Ops:
  285.1 8.9 %copy-start = (bf16[8,144,896]{2,1,0:T(8,128)(2,1)S(1)}, bf16[8,144,896]{2,1,0:T(8,128)(2,1)}, u32[]{:S(2)}) copy-start(bf16[8,144,896]{2,1,0:T(8,128)(2,1)} %get-tuple-element.20) | copy-start | bytes 6193156
  326.0 8.0 %copy-start.1 = (bf16[2,144,1152]{2,1,0:T(8,128)(2,1)S(1)}, bf16[2,144,1152]{2,1,0:T(8,128)(2,1)}, u32[]{:S(2)}) copy-start(bf16[2,144,1152]{2,1,0:T(8,128)(2,1)} %get-tuple-element.21) | copy-start | bytes 1990660
  334.8 4.2 %copy-start.2 = (bf16[256,1120]{1,0:T(8,128)(2,1)S(1)}, bf16[256,1120]{1,0:T(8,128)(2,1)}, u32[]{:S(2)}) copy-start(bf16[256,1120]{1,0:T(8,128)(2,1)} %get-tuple-element.18) | copy-start | bytes 1720324

commit v3 on v2

--- a/solution.py
+++ b/solution.py
@@ -44,11 +44,11 @@
 
 def layer_kernel(
     dim, ff,
-    tok_h, dy_h, wq_h, wo_h, wf_h, wp_h, len_s, lnv,
+    tok_h, dy_h, wq_h, wo_h, wf_h, wp_h, len_s, g1_i, b1_i, g2_i, b2_i,
     res_o, gtok_o, gq_o, go_o, gf_o, gp_o, gln_o,
     tok, dys, xown, wq, wo, wf, wp, first, qs, ks, vs, pm, att, part, ra, sb, rb, mix, dmix,
     sec, act, gel, datt, dqkv, gq, go, gf, gp, yq, yo, yf, yp, zq, zo, zf, zp,
-    lnr, vec, lens, lg, lr, lz,
+    lnv, lnr, vec, lens, lg, lr, lz,
     raw_sem, ag_sem, rs_sem, fin_sem, xs_sem, xa_sem, ln_sem,
 ):
     blk = dim // NZ
@@ -377,7 +377,7 @@
 
     base = pl.multiple_of(bp * z, 16)
 
-    def prepare(rq, rt, ro, rd):
+    def prepare(rq, rt, ro, rd, turned):
         loads = [
             pltpu.make_async_copy(wq_h, rq, raw_sem.at[0]),
             pltpu.make_async_copy(tok_h, rt, raw_sem.at[1]),
@@ -386,6 +386,9 @@
         ]
         for load in loads:
             load.start()
+        lnv[...] = jnp.zeros_like(lnv)
+        for k, ref in enumerate((g1_i, b1_i, g2_i, b2_i)):
+            lnv[k : k + 1, 0:blk] = ref[...].astype(F32).reshape(1, blk)
         lnr[z] = lnv[...]
         for k in range(1, NZ):
             send(lambda k=k: remote(lnv, lnr.at[z], ln_sem.at[k - 1], ln_sem.at[2 + k], others[k - 1]))
@@ -399,14 +402,16 @@
                     wq[pl.ds(base, blk), blk * j : blk * (j + 1)] = rq[:, dim * j + blk * k : dim * j + blk * (k + 1)]
         ag_start("q")
 
+        turned[...] = jnp.zeros_like(turned)
+
         def spread(dst, src):
-            dst[...] = jnp.zeros((SEQ, dp), BF)
             for j in range(NZ):
-                dst[:, bp * j : bp * j + blk] = src[:, blk * j : blk * (j + 1)]
+                turned[bp * j : bp * j + blk, :] = src[blk * j : blk * (j + 1), :]
+            dst[...] = turned[...].T
 
         loads[1].wait()
         for s in range(WAVES):
-            spread(xown.at[s], rt.at[pl.ds(SEQ * s, SEQ)])
+            spread(xown.at[s], rt.at[s])
             sent = jnp.where(lane == blk, len_s[s].astype(F32), xown[s].astype(F32))
             tok[blk_of(s, c, x)] = sent.astype(BF)
             xg_start(tok, 0, s, track=False)
@@ -420,7 +425,7 @@
         ag_start("o")
         loads[3].wait()
         for s in range(WAVES):
-            spread(dys.at[blk_of(s, c, x)], rd.at[pl.ds(SEQ * s, SEQ)])
+            spread(dys.at[blk_of(s, c, x)], rd.at[s])
             xg_start(dys, 1, s)
 
     def prepare_mlp(rf, rp):
@@ -446,9 +451,10 @@
     pl.run_scoped(
         prepare,
         pltpu.VMEM((blk, 3 * dim), BF),
-        pltpu.VMEM((WAVES * SEQ, dim), BF),
+        pltpu.VMEM((WAVES, dim, SEQ), BF),
         pltpu.VMEM((blk, dim), BF),
-        pltpu.VMEM((WAVES * SEQ, dim), BF),
+        pltpu.VMEM((WAVES, dim, SEQ), BF),
+        pltpu.VMEM((dp, SEQ), BF),
     )
     pl.run_scoped(prepare_mlp, pltpu.VMEM((blk, ff), BF), pltpu.VMEM((blk, dim), BF))
 
@@ -704,9 +710,7 @@
         rs_stage("f", d, 1)
 
     for s in range(WAVES):
-        rows = (mix[s] + ex_sum(1, s)).astype(BF)
-        for j in range(NZ):
-            res_o[SEQ * s : SEQ * (s + 1), blk * j : blk * (j + 1)] = rows[:, bp * j : bp * j + blk]
+        res_o[s] = (mix[s] + ex_sum(1, s)).astype(BF)
     ex_sent(1)
     for s in range(WAVES):
         matmul_part(dqkv, wq, s, True)
@@ -729,9 +733,7 @@
         n, inv = stats(xown[s].astype(F32))
         lg[0:1, :] = lg[0:1, :] + jnp.sum(d1 * n, axis=0, keepdims=True)
         lg[1:2, :] = lg[1:2, :] + jnp.sum(d1, axis=0, keepdims=True)
-        rows = (dmix[s] + norm_back(d1 * vec[0:1, :], n, inv)).astype(BF)
-        for j in range(NZ):
-            gtok_o[SEQ * s : SEQ * (s + 1), blk * j : blk * (j + 1)] = rows[:, bp * j : bp * j + blk]
+        gtok_o[s] = (dmix[s] + norm_back(d1 * vec[0:1, :], n, inv)).astype(BF)
 
     back_first(0)
     back_first(1)
@@ -775,13 +777,12 @@
             pl.when(cond())(lambda make=make: make().wait_send())
 
 
-def layer_call(dim, ff, tokens, cot, w_qkv, w_out, w_fc, w_proj, lengths, lnv):
+def layer_call(dim, ff, tokens, cot, w_qkv, w_out, w_fc, w_proj, lengths, norms):
     blk = dim // NZ
     bp = up16(blk)
     hb = bp // 2
     dp = NZ * bp
     nq = up128(3 * blk)
-    rows = WAVES * SEQ
     vm, dma = pltpu.VMEM, pltpu.SemaphoreType.DMA
     big = (NB, SEQ, dp)
     scratch = [
@@ -799,7 +800,7 @@
         vm((dp, nq), BF), vm((bp, dp), BF), vm((dp, dp), BF), vm((dp, dp), BF),
         vm((NZ, hb, nq), BF), vm((1, hb, dp), BF), vm((NZ, hb, dp), BF), vm((NZ, hb, dp), BF),
         vm((NZ + 1, hb, nq), BF), vm((2, hb, dp), BF), vm((NZ + 1, hb, dp), BF), vm((NZ + 1, hb, dp), BF),
-        vm((NZ, 8, up128(blk)), F32), vm((8, dp), F32), vm((NB, 8, SEQ), F32),
+        vm((8, up128(blk)), F32), vm((NZ, 8, up128(blk)), F32), vm((8, dp), F32), vm((NB, 8, SEQ), F32),
         vm((8, dp), F32), vm((3, 8, dp), F32), vm((3, 8, dp), F32),
         dma((6,)), dma((17, 5)), dma((4, 17)), dma((4, 16)), dma((8, 6)), dma((8, 4)), dma((18,)),
     ]
@@ -813,17 +814,68 @@
     return pl.pallas_call(
         body,
         out_shape=(
-            shape((rows, dim), BF), shape((rows, dim), BF),
+            shape((WAVES, SEQ, dp), BF), shape((WAVES, SEQ, dp), BF),
             shape((8, hb, nq), BF), shape((2, hb, dp), BF), shape((8, hb, dp), BF), shape((8, hb, dp), BF),
             shape((8, up128(blk)), F32),
         ),
-        in_specs=[hbm] * 6 + [pl.BlockSpec(memory_space=pltpu.SMEM), inv],
+        in_specs=[hbm] * 6 + [pl.BlockSpec(memory_space=pltpu.SMEM)] + [inv] * 4,
         out_specs=(inv, inv, hbm, hbm, hbm, hbm, inv),
         scratch_shapes=scratch,
         compiler_params=pltpu.CompilerParams(
             collective_id=0, has_side_effects=True, vmem_limit_bytes=67043328
         ),
-    )(tokens, cot, w_qkv, w_out, w_fc, w_proj, lengths, lnv)
+    )(tokens, cot, w_qkv, w_out, w_fc, w_proj, lengths, *norms)
+
+
+def finish_kernel(dim, ff, res, gtok, gq, go, gf, gp, gln, res_o, gtok_o, gq_o, go_o, gf_o, gp_o, *norms_o):
+    blk = dim // NZ
+    bp = up16(blk)
+    for j in range(NZ):
+        there = slice(bp * j, bp * j + blk)
+        go_o[:, blk * j : blk * (j + 1)] = go[:, there].astype(F32)
+        for t in range(NT):
+            gp_o[t, :, blk * j : blk * (j + 1)] = gp[t, :, there].astype(F32)
+            lo = (ff // NZ) * j + blk * t
+            gf_o[:, lo : lo + blk] = gf[t, :, there].astype(F32)
+    for j in range(3):
+        for t in range(NT):
+            lo = dim * j + blk * t
+            gq_o[:, lo : lo + blk] = gq[t, :, blk * j : blk * (j + 1)].astype(F32)
+
+    @pl.when(pl.program_id(0) == 0)
+    def _():
+        for k, ref in enumerate(norms_o):
+            ref[...] = gln[k : k + 1, 0:blk].reshape(blk)
+        for src, dst in ((res, res_o), (gtok, gtok_o)):
+            for s in range(WAVES):
+                turned = src[s].T
+                for j in range(NZ):
+                    dst[s, blk * j : blk * (j + 1), :] = turned[bp * j : bp * j + blk, :]
+
+
+def finish_call(dim, ff, res, gtok, gq, go, gf, gp, gln):
+    blk = dim // NZ
+    bp = up16(blk)
+    dp = NZ * bp
+    nq = gq.shape[2]
+    step = 56
+    shape, spec = jax.ShapeDtypeStruct, pl.BlockSpec
+    whole = spec(memory_space=pltpu.VMEM)
+    quarters = lambda n: spec((NT, step, n), lambda i: (0, i, 0))
+    lines = lambda n: spec((step, n), lambda i: (i, 0))
+    return pl.pallas_call(
+        lambda *refs: finish_kernel(dim, ff, *refs),
+        grid=(blk // step,),
+        in_specs=[whole, whole, quarters(nq), lines(dp), quarters(dp), quarters(dp), whole],
+        out_specs=[whole, whole, lines(3 * dim), lines(dim), lines(ff), quarters(dim)] + [whole] * 4,
+        out_shape=[
+            shape((WAVES, dim, SEQ), BF), shape((WAVES, dim, SEQ), BF),
+            shape((blk, 3 * dim), F32), shape((blk, dim), F32), shape((blk, ff), F32), shape((NT, blk, dim), F32),
+        ] + [shape((blk,), F32)] * 4,
+        compiler_params=pltpu.CompilerParams(vmem_limit_bytes=67043328),
+    )(
+        res, gtok, gq.reshape(NT, bp, nq), go.reshape(bp, dp), gf.reshape(NT, bp, dp), gp.reshape(NT, bp, dp), gln
+    )
 
 
 def sum_boxes(value, wide):
@@ -843,24 +895,14 @@
         ff = w_fc.shape[1]
         blk = dim // NZ
         bp = up16(blk)
-        lnv = jnp.pad(
-            jnp.stack([ln1_gain, ln1_bias, ln2_gain, ln2_bias]).astype(F32), ((0, 4), (0, up128(blk) - blk))
+        res, gtok, gq, go, gf, gp, gln = layer_call(
+            dim, ff, tokens.transpose(0, 2, 1), cotangent.transpose(0, 2, 1),
+            w_qkv, w_out, w_fc, w_proj, lengths, (ln1_gain, ln1_bias, ln2_gain, ln2_bias),
         )
-        res, gtok, gq, go, gf, gp, gln = layer_call(
-            dim, ff, tokens.reshape(cells * seq, dim), cotangent.reshape(cells * seq, dim),
-            w_qkv, w_out, w_fc, w_proj, lengths, lnv,
-        )
-        gq = gq.reshape(NT, bp, gq.shape[2])[:, :blk, : 3 * blk].astype(F32)
-        gq = gq.reshape(NT, blk, 3, blk).transpose(1, 2, 0, 3).reshape(blk, 3 * dim)
-        go = go.reshape(bp, NZ, bp)[:blk, :, :blk].astype(F32).reshape(blk, dim)
-        gf = gf.reshape(NT, bp, NZ, bp)[:, :blk, :, :blk].astype(F32)
-        gf = gf.transpose(1, 2, 0, 3).reshape(blk, ff)
-        gp = gp.reshape(NT, bp, NZ, bp)[:, :blk, :, :blk].astype(F32).reshape(NT * blk, dim)
-        grads = [sum_boxes(g, wide) for g in (gq, go, gf, gp, gln)]
-        gq, go, gf, gp, gln = grads
+        res, gtok, *grads = finish_call(dim, ff, res, gtok, gq, go, gf, gp, gln)
+        gq, go, gf, gp, g1, b1, g2, b2 = [sum_boxes(g, wide) for g in grads]
         return (
-            res.reshape(cells, seq, dim), gtok.reshape(cells, seq, dim),
-            gln[0, :blk], gln[1, :blk], gq, go, gln[2, :blk], gln[3, :blk], gf, gp,
+            res.transpose(0, 2, 1), gtok.transpose(0, 2, 1), g1, b1, gq, go, g2, b2, gf, gp.reshape(ff // NZ, dim)
         )
 
     rows = P(("wide", "narrow"), None, None)

time: 345 us -> 273 us (0.79); the launches traced: 340 us -> 272 us
  local copies, waits for them, and re-layouts: 70.6 us -> 0 us
  Pallas kernels: 261 us -> 272 us
  other arithmetic: 8.08 us -> 0 us
    reshape x9 -> x0, local copies, waits for them, and re-layouts: 54.4 us -> none  [the longest x2 16.2 us: shards(): gf = gf.transpose(1, 2, 0, 3).reshape(blk, ff)]
    pallas_call x1 -> x2, Pallas kernels: 261 us -> 272 us  [the longest x1 261 us: layer_call(): pl.pallas_call(body, out_shape=(shape((WAVES, SEQ, dp), BF), shape((WAVES...]
    unnamed x11 -> x0, local copies, waits for them, and re-layouts: 10.5 us -> none
    reshape x4 -> x0, other arithmetic: 7.46 us -> none  [the longest x1 3.69 us: shards(): gp.reshape(NT, bp, NZ, bp)[:, :blk, :, :blk].astype(F32)]
where the time goes in v3:
time: 273 us; the launch traced here: 272 us
  Pallas kernels  272 us (100%)
    pallas_call x1, Pallas kernels, layer_call(): pl.pallas_call(body, out_shape=(shape((WAVES, SEQ, dp), BF), shape((WAVES...  261 us
    pallas_call x1, Pallas kernels, finish_call(): pl.pallas_call(lambda *refs: finish_kernel(dim, ff, *refs), grid=(blk //...  11.1 us

profile of v3, /device:TPU:0, one launch (start us, length us, event | category | flops | bytes accessed | tf_op | source)
XLA Modules:
  0.0 272.5 jit_solution(14480888216737466565)
XLA Ops:
  0.6 260.5 %shard_map.186 = (bf16[2,128,1152]{2,1,0:T(8,128)(2,1)}, bf16[2,128,1152]{2,1,0:T(8,128)(2,1)}, bf16[8,144,896]{2,1,0:T(8,128)(2,1)}, bf16[2,144,1152]{2,1,0:T(8...) custom-call(bf16[2,1120,128]{2,1,0:T(8,128)(2,1)} %bitcast.13, ...), custom_call_target="tpu_custom_call" | custom-call | tf_op jit(solution)/shard_map/pallas_call | solution.py:814
  261.2 11.1 %shard_map.187 = (bf16[2,1120,128]{2,1,0:T(8,128)(2,1)}, bf16[2,1120,128]{2,1,0:T(8,128)(2,1)}, f32[280,3360]{1,0:T(8,128)}, f32[280,1120]{1,0:T(8,128)}, f32[28...) custom-call(bf16[2,128,1152]{2,1,0:T(8,128)(2,1)} %get-tuple-element.2, ...), custom_call_target="tpu_custom_call" | custom-call | tf_op jit(solution)/shard_map/pallas_call | solution.py:866

commit v4 on v3

--- a/solution.py
+++ b/solution.py
@@ -20,6 +20,7 @@
 NB = NT * WAVES
 GELU_C = math.sqrt(2.0 / math.pi)
 GELU_A = 0.044715
+ZFIRST = ("p",)
 
 
 def up16(n):
@@ -46,7 +47,7 @@
     dim, ff,
     tok_h, dy_h, wq_h, wo_h, wf_h, wp_h, len_s, g1_i, b1_i, g2_i, b2_i,
     res_o, gtok_o, gq_o, go_o, gf_o, gp_o, gln_o,
-    tok, dys, xown, wq, wo, wf, wp, first, qs, ks, vs, pm, att, part, ra, sb, rb, mix, dmix,
+    tok, dys, xown, wq, wo, wf, wp, qs, ks, vs, att, part, part1, ra, sb, rb, mix, dmix,
     sec, act, gel, datt, dqkv, gq, go, gf, gp, yq, yo, yf, yp, zq, zo, zf, zp,
     lnv, lnr, vec, lens, lg, lr, lz,
     raw_sem, ag_sem, rs_sem, fin_sem, xs_sem, xa_sem, ln_sem,
@@ -191,10 +192,13 @@
         for kind in ("x", "own", "fwd"):
             xg(ref, e, s, kind).wait_send()
 
+    def part_of(e):
+        return part1 if e == 1 else part
+
     def ex_a(e, s):
         i = 2 * e + s
         return remote(
-            part.at[pl.ds(s * NT + (1 - c) * 2, 2)], ra.at[int(e == 1), s],
+            part_of(e).at[pl.ds(s * NT + (1 - c) * 2, 2)], ra.at[int(e == 1), s],
             xa_sem.at[i, 0], xa_sem.at[i, 1], core_dev,
         )
 
@@ -205,34 +209,36 @@
     def ex_relay(e, s):
         ex_a(e, s).wait_recv()
         sb[int(e == 1), s] = (
-            part[blk_of(s, c, 1 - x)].astype(F32) + ra[int(e == 1), s, 1 - x].astype(F32)
+            part_of(e)[blk_of(s, c, 1 - x)].astype(F32) + ra[int(e == 1), s, 1 - x].astype(F32)
         ).astype(BF)
         ex_b(e, s).start()
 
     def ex_sum(e, s):
         ex_b(e, s).wait_recv()
         return (
-            part[blk_of(s, c, x)].astype(F32)
+            part_of(e)[blk_of(s, c, x)].astype(F32)
             + ra[int(e == 1), s, x].astype(F32)
             + rb[int(e == 1), s].astype(F32)
         )
 
-    def ex_sent(e):
-        for s in range(WAVES):
-            ex_a(e, s).wait_send()
-            ex_b(e, s).wait_send()
-
+    base = pl.multiple_of(bp * z, 16)
     reduces = {"q": (gq, yq, zq, 0), "f": (gf, yf, zf, 1), "p": (gp, yp, zp, 2), "o": (go, yo, zo, 3)}
 
     def rs_y(name, d):
         g, yr, zr, i = reduces[name]
         if name == "o":
             return remote(g.at[rows_of(0, 1 - y)], yr.at[0], rs_sem.at[i, 0], rs_sem.at[i, 4], y_dev)
+        if name in ZFIRST:
+            return remote(g.at[rows_of(z, 1 - y)], yr.at[0], rs_sem.at[i, 0], rs_sem.at[i, 4], y_dev)
         return remote(g.at[rows_of(d, 1 - y)], yr.at[d], rs_sem.at[i, d], rs_sem.at[i, 4 + d], y_dev)
 
     def rs_z(name, d, slot, up):
         g, yr, zr, i = reduces[name]
         dd = 0 if name == "o" else d
+        if name in ZFIRST:
+            return remote(
+                g.at[pl.ds(bp * d, bp)], zr.at[slot], rs_sem.at[i, 8 + d], rs_sem.at[i, 12 + slot], up_dev if up else down_dev
+            )
         return remote(yr.at[dd], zr.at[slot], rs_sem.at[i, 8 + dd], rs_sem.at[i, 12 + slot], up_dev if up else down_dev)
 
     def add_up(dst, srcs):
@@ -246,7 +252,7 @@
             dst[r, :] = total.astype(BF)
             return carry
 
-        lax.fori_loop(0, hb // step, body, 0)
+        lax.fori_loop(0, dst.shape[0] // step, body, 0)
 
     def rs_start(name, dests=(3, 0, 2, 1)):
         for d in (0,) if name == "o" else dests:
@@ -257,6 +263,12 @@
 
         def side(pos, up):
             def run():
+                if name in ZFIRST:
+                    if j > 0:
+                        own = g.at[pl.ds(bp * d, bp)]
+                        rs_z(name, d, d, up).wait_recv()
+                        add_up(own, [own, zr.at[d]])
+                    return
                 rs_y(name, d).wait_recv()
                 own = g.at[rows_of(0 if name == "o" else d, y)]
                 mine = yr.at[0 if name == "o" else d]
@@ -293,8 +305,27 @@
         if NZ - 1 - j > d:
             side(NZ - 1 - j, False)
 
+    def rs_line(name):
+        g, yr, zr, i = reduces[name]
+        own = g.at[pl.ds(base, bp)]
+
+        def run(slots):
+            def go_():
+                for slot in slots:
+                    rs_z(name, slot if slot < NZ else 0, slot, True).wait_recv()
+                add_up(own, [own] + [zr.at[slot] for slot in slots])
+            return go_
+
+        for k in range(NZ):
+            pl.when(z == k)(run(([k] if k < NZ - 1 else []) + ([NZ] if k > 0 else [])))
+        send(lambda: rs_y(name, 0))
+
     def rs_final(name):
         g, yr, zr, i = reduces[name]
+        if name in ZFIRST:
+            rs_y(name, 0).wait_recv()
+            add_up(yr.at[0], [g.at[rows_of(z, y)], yr.at[0]])
+            return
         out = name == "o"
         me = 0 if out else z
         here = (t == z) if out else (z >= 0)
@@ -330,7 +361,7 @@
 
     def own_block(name):
         yr = reduces[name][1]
-        return yr.at[0] if name == "o" else yr.at[z]
+        return yr.at[0] if name == "o" or name in ZFIRST else yr.at[z]
 
     def keep_own(name):
         return pltpu.make_async_copy(own_block(name), fin_view(name, t, y), fin_sem.at[reduces[name][3], 7])
@@ -357,9 +388,9 @@
         send(lambda: fin_copy(name, v, t, 1 - y, 3, x_dev), lambda: here)
         send(lambda: fin_copy(name, v, t, 1 - y, 4, core_dev), lambda: here)
 
-    def fin_forward_x(name):
+    def fin_forward_x(name, other):
         here = (tx == z) if name == "o" else (z >= 0)
-        for k, yy in ((5, y), (6, 1 - y)):
+        for k, yy in ((6, 1 - y) if other else (5, y),):
             pl.when(here)(lambda yy=yy: fin_wait(name, tx, yy))
             send(lambda k=k, yy=yy: fin_copy(name, fin_view(name, tx, yy), tx, yy, k, core_dev), lambda: here)
 
@@ -374,8 +405,6 @@
                 for yy in range(2):
                     fin_wait(name, 2 * xx + (1 - c), yy)
             keep_own(name).wait()
-
-    base = pl.multiple_of(bp * z, 16)
 
     def prepare(rq, rt, ro, rd, turned):
         loads = [
@@ -458,323 +487,368 @@
     )
     pl.run_scoped(prepare_mlp, pltpu.VMEM((blk, ff), BF), pltpu.VMEM((blk, dim), BF))
 
-    for k in range(1, NZ):
-        remote(lnv, lnr.at[lax.rem(z + NZ - k, NZ)], ln_sem.at[k - 1], ln_sem.at[2 + k], others[k - 1]).wait_recv()
-    vec[...] = jnp.zeros_like(vec)
-    for j in range(NZ):
-        vec[:, bp * j : bp * j + blk] = lnr[j, :, 0:blk]
-    lg[...] = jnp.zeros_like(lg)
-    dqkv[...] = jnp.zeros_like(dqkv)
-
-    def stats(rows):
-        mean = jnp.sum(rows, axis=-1, keepdims=True) * inv_dim
-        cen = (rows - mean) * livef
-        inv = lax.rsqrt(jnp.sum(cen * cen, axis=-1, keepdims=True) * inv_dim + EPS)
-        return cen * inv, inv
-
-    def norm_back(e, n, inv):
-        me = jnp.sum(e, axis=-1, keepdims=True) * inv_dim
-        mn = jnp.sum(e * n, axis=-1, keepdims=True) * inv_dim
-        return inv * (e - me - n * mn) * livef
-
-    def ln_first(s):
-        def body(i, carry):
-            b = s * NT + i
-            raw = tok[b].astype(F32)
-            lens[b] = jnp.broadcast_to(raw[0:8, blk : blk + 1], (8, SEQ))
-            n, inv = stats(raw * livef)
-            first[b] = (n * vec[0:1, :] + vec[1:2, :]).astype(BF)
-            return carry
-        lax.fori_loop(0, NT, body, 0)
-
-    lane_h = lax.broadcasted_iota(jnp.int32, (1, bp), 1)
-    head_masks = [(lane_h >= head * h) & (lane_h < head * (h + 1)) for h in range(nh)]
-
-    def stack_heads(v):
-        zero = jnp.zeros_like(v)
-        return jnp.concatenate([jnp.where(m, v, zero) for m in head_masks], axis=0)
-
-    def side_by_side(v):
-        return jnp.concatenate([v[SEQ * h : SEQ * (h + 1)] for h in range(nh)], axis=1)
-
-    def project(s):
-        def body(i, carry):
-            b = s * NT + i * 2
-            rows = first[pl.ds(b, 2)].reshape(2 * SEQ, dp)
-            out = nn(rows, wq[...])
-            for j, ref in enumerate((qs, ks, vs)):
-                ref[pl.ds(b, 2)] = out[:, blk * j : blk * j + bp].astype(BF).reshape(2, SEQ, bp)
-            return carry
-        lax.fori_loop(0, 2, body, 0)
-
-    def attend(s):
-        q_pos = lax.broadcasted_iota(jnp.int32, (SEQ, SEQ), 0)
-        k_pos = lax.broadcasted_iota(jnp.int32, (SEQ, SEQ), 1)
-
-        def body(i, carry):
-            b = s * NT + i
-            scores = nt(stack_heads(qs[b]), ks[b]) * scale
-            ok = (k_pos <= q_pos) & (k_pos.astype(F32) < lens[b, 0:1, :])
-            bias = jnp.concatenate([ok.astype(F32)] * nh, axis=0) > 0.5
-            scores = jnp.where(bias, scores, MASKED)
-            top = jnp.max(scores, axis=-1, keepdims=True)
-            ex = jnp.exp(scores - top)
-            prob = ex / jnp.sum(ex, axis=-1, keepdims=True)
-            pm[b] = prob
-            out = nn(side_by_side(prob.astype(BF)), stack_heads(vs[b]))
-            att[b] = out.astype(BF)
-            return carry
-        lax.fori_loop(0, NT, body, 0)
-
-    def matmul_part(src, weight, s, transposed):
-        width = src.shape[2]
-
-        def body(i, carry):
-            b = s * NT + i * 2
-            rows = src[pl.ds(b, 2)].reshape(2 * SEQ, width)
-            out = nt(rows, weight[...]) if transposed else nn(rows, weight[...])
-            part[pl.ds(b, 2)] = out.astype(BF).reshape(2, SEQ, dp)
-            return carry
-        lax.fori_loop(0, 2, body, 0)
-
-    ag_forward("q", 1)
-    xg_forward(tok, 0, 0, track=False)
-    ag_forward("q", 2)
-    ag_start("f")
-    ag_forward("o", 1)
-    xg_finish(tok, 0, 0)
-    ln_first(0)
-    xg_forward(tok, 0, 1, track=False)
-    ag_forward("q", 3)
-    xg_finish(tok, 0, 1)
-    ln_first(1)
-    ag_forward("o", 2)
-    ag_start("p")
-    ag_forward("f", 1)
-    ag_forward("o", 3)
-    ag_finish("q")
-    project(0)
-    attend(0)
-    ag_finish("o")
-    matmul_part(att, wo, 0, False)
-    ex_a(0, 0).start()
-    ag_forward("f", 2)
-    project(1)
-    attend(1)
-    matmul_part(att, wo, 1, False)
-    ex_a(0, 1).start()
-    ex_relay(0, 0)
-    ag_forward("f", 3)
-    ag_forward("p", 1)
-    ex_relay(0, 1)
-    xg_forward(dys, 1, 0)
-    xg_forward(dys, 1, 1)
-
-    def mid(s):
-        rows = xown[s].astype(F32) + ex_sum(0, s)
-        mix[s] = rows
-        n, inv = stats(rows)
-        sec[blk_of(s, c, x)] = (n * vec[2:3, :] + vec[3:4, :]).astype(BF)
-        xg_start(sec, 2, s)
-
-    mid(0)
-    mid(1)
-    ag_forward("p", 2)
-    xg_forward(sec, 2, 0)
-    xg_forward(sec, 2, 1)
-    ag_forward("p", 3)
-    for s in range(WAVES):
-        xg_sent(tok, 0, s)
-    ex_sent(0)
-    ag_finish("f")
-
-    def expand(s):
-        def body(i, carry):
-            b = s * NT + i * 2
-            rows = sec[pl.ds(b, 2)].reshape(2 * SEQ, dp)
-            pre = nn(rows, wf[...])
-            sq = pre * pre
-            th = jnp.tanh(GELU_C * (pre + GELU_A * (pre * sq)))
-            half = 0.5 * (1.0 + th)
-            act[pl.ds(b, 2)] = (pre * half).astype(BF).reshape(2, SEQ, dp)
-            slope = half + (0.5 * GELU_C) * pre * (1.0 - th * th) * (1.0 + (3.0 * GELU_A) * sq)
-            gel[pl.ds(b, 2)] = slope.astype(BF).reshape(2, SEQ, dp)
-            return carry
-        lax.fori_loop(0, 2, body, 0)
-
-    for s in range(WAVES):
-        xg_finish(sec, 2, s)
-        expand(s)
-    for s in range(WAVES):
-        xg_finish(dys, 1, s)
-
-    def grad_of(dst, left, right):
-        step = 384
-        rows = NB * SEQ
-
-        def body(j, carry):
-            cols = pl.ds(pl.multiple_of(j * step, step), step)
-            out = tn(left[:, :, cols].reshape(rows, step), right[...].reshape(rows, right.shape[2]))
-            dst[cols, :] = out.astype(BF)
-            return carry
-        lax.fori_loop(0, dp // step, body, 0)
-
-    grad_of(gp, act, dys)
-    rs_start("p")
-    ag_finish("p")
-
-    def back_act(s):
-        def body(i, carry):
-            b = s * NT + i * 2
-            d_act = nt(dys[pl.ds(b, 2)].reshape(2 * SEQ, dp), wp[...])
-            slope = gel[pl.ds(b, 2)].reshape(2 * SEQ, dp).astype(F32)
-            gel[pl.ds(b, 2)] = (d_act * slope).astype(BF).reshape(2, SEQ, dp)
-            return carry
-        lax.fori_loop(0, 2, body, 0)
-
-    for s in range(WAVES):
-        back_act(s)
-        matmul_part(gel, wf, s, True)
-        ex_a(2, s).start()
-    rs_stage("p", 3, 0)
-    rs_stage("p", 0, 0)
-    ex_relay(2, 0)
-    ex_relay(2, 1)
-    grad_of(gf, sec, gel)
-    rs_start("f")
-    for d in (2, 1):
-        rs_stage("p", d, 0)
-    for d in (3, 0):
-        rs_stage("p", d, 1)
-
-    def back_mid(s):
-        d2 = ex_sum(2, s)
-        n, inv = stats(mix[s])
-        lg[2:3, :] = lg[2:3, :] + jnp.sum(d2 * n, axis=0, keepdims=True)
-        lg[3:4, :] = lg[3:4, :] + jnp.sum(d2, axis=0, keepdims=True)
-        rows = dys[blk_of(s, c, x)].astype(F32) + norm_back(d2 * vec[2:3, :], n, inv)
-        dmix[s] = rows
-        tok[blk_of(s, c, x)] = rows.astype(BF)
-        xg_start(tok, 3, s)
-
-    back_mid(0)
-    back_mid(1)
-    ex_sent(2)
-    for d in (2, 1):
-        rs_stage("p", d, 1)
-    for d in (3, 0):
-        rs_stage("p", d, 2)
-    for s in range(WAVES):
-        matmul_part(act, wp, s, False)
-        ex_a(1, s).start()
-    xg_forward(tok, 3, 0)
-    xg_forward(tok, 3, 1)
-    ex_relay(1, 0)
-    ex_relay(1, 1)
-    rs_final("p")
-    fin_start("p")
-
-    def back_attend(s):
-        def proj(i, carry):
-            b = s * NT + i * 2
-            out = nt(tok[pl.ds(b, 2)].reshape(2 * SEQ, dp), wo[...])
-            datt[pl.ds(b, 2)] = out.astype(BF).reshape(2, SEQ, bp)
-            return carry
-        lax.fori_loop(0, 2, proj, 0)
-
-        def body(i, carry):
-            b = s * NT + i
-            d_out = stack_heads(datt[b])
-            prob = pm[b]
-            d_prob = nt(d_out, vs[b])
-            total = jnp.sum(prob * d_prob, axis=-1, keepdims=True)
-            d_scores = (prob * (d_prob - total)).astype(BF)
-            dqkv[b, :, 0:bp] = (nn(side_by_side(d_scores), stack_heads(ks[b])) * scale).astype(BF)
-            dqkv[b, :, blk : blk + bp] = (tn(d_scores, stack_heads(qs[b])) * scale).astype(BF)
-            dqkv[b, :, 2 * blk : 2 * blk + bp] = tn(prob.astype(BF), d_out).astype(BF)
-            return carry
-        lax.fori_loop(0, NT, body, 0)
-
-    xg_finish(tok, 3, 0)
-    back_attend(0)
-    for d in (3, 0, 2, 1):
-        rs_stage("f", d, 0)
-    xg_finish(tok, 3, 1)
-    back_attend(1)
-    rows_all = NB * SEQ
-    go[...] = tn(att[...].reshape(rows_all, bp), tok[...].reshape(rows_all, dp)).astype(BF)
-    rs_start("o")
-    grad_of(gq, first, dqkv)
-    rs_start("q")
-    for d in (3, 0, 2, 1):
-        rs_stage("f", d, 1)
-
-    for s in range(WAVES):
-        res_o[s] = (mix[s] + ex_sum(1, s)).astype(BF)
-    ex_sent(1)
-    for s in range(WAVES):
-        matmul_part(dqkv, wq, s, True)
-        ex_a(3, s).start()
-    for d in (3, 0):
-        rs_stage("f", d, 2)
-    ex_relay(3, 0)
-    ex_relay(3, 1)
-    rs_final("f")
-    fin_start("f")
-    fin_forward_y("p")
-    rs_stage("o", 0, 0)
-    fin_forward_x("p")
-    rs_stage("o", 0, 1)
-    for d in (3, 0, 2, 1):
-        rs_stage("q", d, 0)
-
-    def back_first(s):
-        d1 = ex_sum(3, s)
-        n, inv = stats(xown[s].astype(F32))
-        lg[0:1, :] = lg[0:1, :] + jnp.sum(d1 * n, axis=0, keepdims=True)
-        lg[1:2, :] = lg[1:2, :] + jnp.sum(d1, axis=0, keepdims=True)
-        gtok_o[s] = (dmix[s] + norm_back(d1 * vec[0:1, :], n, inv)).astype(BF)
-
-    back_first(0)
-    back_first(1)
-    ex_sent(3)
-    rs_stage("o", 0, 2)
-    for d in (3, 0, 2, 1):
-        rs_stage("q", d, 1)
-    rs_final("o")
-    fin_start("o")
-    fin_forward_y("f")
-    fin_forward_x("f")
-
-    for k, dev in enumerate((core_dev, x_dev, y_dev)):
-        hop = remote(lg, lr.at[k], ln_sem.at[6 + 2 * k], ln_sem.at[7 + 2 * k], dev)
-        hop.start()
-        hop.wait()
-        lg[...] = lg[...] + lr[k]
-    for k in range(1, NZ):
-        send(lambda k=k: remote(lg, lz.at[k - 1], ln_sem.at[11 + k], ln_sem.at[14 + k], others[k - 1]))
-    for d in (3, 0):
-        rs_stage("q", d, 2)
-    rs_final("q")
-    fin_start("q")
-    fin_forward_y("o")
-    for k in range(1, NZ):
-        remote(lg, lz.at[k - 1], ln_sem.at[11 + k], ln_sem.at[14 + k], others[k - 1]).wait_recv()
-    total = lg[...] + lz[0] + lz[1] + lz[2]
-    for j in range(NZ):
-        @pl.when(z == j)
-        def _(j=j):
-            gln_o[:, 0:blk] = total[:, bp * j : bp * j + blk]
-    fin_forward_x("o")
-    fin_forward_y("q")
-    fin_forward_x("q")
-    for name in ("p", "f", "o", "q"):
-        fin_finish(name)
-    for cond, make in ends:
-        if cond is None:
-            make().wait_send()
-        else:
-            pl.when(cond())(lambda make=make: make().wait_send())
+    def main(first, pm):
+        for k in range(1, NZ):
+            remote(lnv, lnr.at[lax.rem(z + NZ - k, NZ)], ln_sem.at[k - 1], ln_sem.at[2 + k], others[k - 1]).wait_recv()
+        vec[...] = jnp.zeros_like(vec)
+        for j in range(NZ):
+            vec[:, bp * j : bp * j + blk] = lnr[j, :, 0:blk]
+        lg[...] = jnp.zeros_like(lg)
+        dqkv[...] = jnp.zeros_like(dqkv)
+
+        def stats(rows):
+            mean = jnp.sum(rows, axis=-1, keepdims=True) * inv_dim
+            cen = (rows - mean) * livef
+            inv = lax.rsqrt(jnp.sum(cen * cen, axis=-1, keepdims=True) * inv_dim + EPS)
+            return cen * inv, inv
+
+        def norm_back(e, n, inv):
+            me = jnp.sum(e, axis=-1, keepdims=True) * inv_dim
+            mn = jnp.sum(e * n, axis=-1, keepdims=True) * inv_dim
+            return inv * (e - me - n * mn) * livef
+
+        def ln_first(s):
+            def body(i, carry):
+                b = s * NT + i
+                raw = tok[b].astype(F32)
+                lens[b] = jnp.broadcast_to(raw[0:8, blk : blk + 1], (8, SEQ))
+                n, inv = stats(raw * livef)
+                first[b] = (n * vec[0:1, :] + vec[1:2, :]).astype(BF)
+                return carry
+            lax.fori_loop(0, NT, body, 0)
+
+        lane_h = lax.broadcasted_iota(jnp.int32, (1, bp), 1)
+        head_masks = [(lane_h >= head * h) & (lane_h < head * (h + 1)) for h in range(nh)]
+
+        def stack_heads(v):
+            zero = jnp.zeros_like(v)
+            return jnp.concatenate([jnp.where(m, v, zero) for m in head_masks], axis=0)
+
+        def side_by_side(v):
+            return jnp.concatenate([v[SEQ * h : SEQ * (h + 1)] for h in range(nh)], axis=1)
+
+        def project(s):
+            def body(i, carry):
+                b = s * NT + i * 2
+                rows = first[pl.ds(b, 2)].reshape(2 * SEQ, dp)
+                out = nn(rows, wq[...])
+                for j, ref in enumerate((qs, ks, vs)):
+                    ref[pl.ds(b, 2)] = out[:, blk * j : blk * j + bp].astype(BF).reshape(2, SEQ, bp)
+                return carry
+            lax.fori_loop(0, 2, body, 0)
+
+        def attend(s):
+            q_pos = lax.broadcasted_iota(jnp.int32, (SEQ, SEQ), 0)
+            k_pos = lax.broadcasted_iota(jnp.int32, (SEQ, SEQ), 1)
+
+            def body(i, carry):
+                b = s * NT + i
+                scores = nt(stack_heads(qs[b]), ks[b]) * scale
+                ok = (k_pos <= q_pos) & (k_pos.astype(F32) < lens[b, 0:1, :])
+                bias = jnp.concatenate([ok.astype(F32)] * nh, axis=0) > 0.5
+                scores = jnp.where(bias, scores, MASKED)
+                top = jnp.max(scores, axis=-1, keepdims=True)
+                ex = jnp.exp(scores - top)
+                prob = ex / jnp.sum(ex, axis=-1, keepdims=True)
+                pm[b] = prob
+                out = nn(side_by_side(prob.astype(BF)), stack_heads(vs[b]))
+                att[b] = out.astype(BF)
+                return carry
+            lax.fori_loop(0, NT, body, 0)
+
+        def matmul_part(src, weight, s, transposed, e):
+            width = src.shape[2]
+            dst = part_of(e)
+
+            def body(i, carry):
+                b = s * NT + i * 2
+                rows = src[pl.ds(b, 2)].reshape(2 * SEQ, width)
+                out = nt(rows, weight[...]) if transposed else nn(rows, weight[...])
+                dst[pl.ds(b, 2)] = out.astype(BF).reshape(2, SEQ, dp)
+                return carry
+            lax.fori_loop(0, 2, body, 0)
+
+        def mid(s):
+            rows = xown[s].astype(F32) + ex_sum(0, s)
+            mix[s] = rows
+            n, inv = stats(rows)
+            sec[blk_of(s, c, x)] = (n * vec[2:3, :] + vec[3:4, :]).astype(BF)
+            xg_start(sec, 2, s)
+
+        def expand(s):
+            def body(i, carry):
+                b = s * NT + i * 2
+                rows = sec[pl.ds(b, 2)].reshape(2 * SEQ, dp)
+                pre = nn(rows, wf[...])
+                sq = pre * pre
+                th = jnp.tanh(GELU_C * (pre + GELU_A * (pre * sq)))
+                half = 0.5 * (1.0 + th)
+                act[pl.ds(b, 2)] = (pre * half).astype(BF).reshape(2, SEQ, dp)
+                slope = half + (0.5 * GELU_C) * pre * (1.0 - th * th) * (1.0 + (3.0 * GELU_A) * sq)
+                gel[pl.ds(b, 2)] = slope.astype(BF).reshape(2, SEQ, dp)
+                return carry
+            lax.fori_loop(0, 2, body, 0)
+
+        def grad_of(dst, left, right):
+            step = 384
+            rows = NB * SEQ
+
+            def body(j, carry):
+                cols = pl.ds(pl.multiple_of(j * step, step), step)
+                out = tn(left[:, :, cols].reshape(rows, step), right[...].reshape(rows, right.shape[2]))
+                dst[cols, :] = out.astype(BF)
+                return carry
+            lax.fori_loop(0, dp // step, body, 0)
+
+        def back_act(s):
+            def body(i, carry):
+                b = s * NT + i * 2
+                d_act = nt(dys[pl.ds(b, 2)].reshape(2 * SEQ, dp), wp[...])
+                slope = gel[pl.ds(b, 2)].reshape(2 * SEQ, dp).astype(F32)
+                gel[pl.ds(b, 2)] = (d_act * slope).astype(BF).reshape(2, SEQ, dp)
+                return carry
+            lax.fori_loop(0, 2, body, 0)
+
+        def back_mid(s):
+            d2 = ex_sum(2, s)
+            n, inv = stats(mix[s])
+            lg[2:3, :] = lg[2:3, :] + jnp.sum(d2 * n, axis=0, keepdims=True)
+            lg[3:4, :] = lg[3:4, :] + jnp.sum(d2, axis=0, keepdims=True)
+            rows = dys[blk_of(s, c, x)].astype(F32) + norm_back(d2 * vec[2:3, :], n, inv)
+            dmix[s] = rows
+            tok[blk_of(s, c, x)] = rows.astype(BF)
+            xg_start(tok, 3, s)
+
+        def back_attend(s):
+            def proj(i, carry):
+                b = s * NT + i * 2
+                out = nt(tok[pl.ds(b, 2)].reshape(2 * SEQ, dp), wo[...])
+                datt[pl.ds(b, 2)] = out.astype(BF).reshape(2, SEQ, bp)
+                return carry
+            lax.fori_loop(0, 2, proj, 0)
+
+            def body(i, carry):
+                b = s * NT + i
+                d_out = stack_heads(datt[b])
+                prob = pm[b]
+                d_prob = nt(d_out, vs[b])
+                total = jnp.sum(prob * d_prob, axis=-1, keepdims=True)
+                d_scores = (prob * (d_prob - total)).astype(BF)
+                dqkv[b, :, 0:bp] = (nn(side_by_side(d_scores), stack_heads(ks[b])) * scale).astype(BF)
+                dqkv[b, :, blk : blk + bp] = (tn(d_scores, stack_heads(qs[b])) * scale).astype(BF)
+                dqkv[b, :, 2 * blk : 2 * blk + bp] = tn(prob.astype(BF), d_out).astype(BF)
+                return carry
+            lax.fori_loop(0, NT, body, 0)
+
+        def back_first(s):
+            d1 = ex_sum(3, s)
+            n, inv = stats(xown[s].astype(F32))
+            lg[0:1, :] = lg[0:1, :] + jnp.sum(d1 * n, axis=0, keepdims=True)
+            lg[1:2, :] = lg[1:2, :] + jnp.sum(d1, axis=0, keepdims=True)
+            gtok_o[s] = (dmix[s] + norm_back(d1 * vec[0:1, :], n, inv)).astype(BF)
+
+        def grad_out():
+            rows_all = NB * SEQ
+            go[...] = tn(att[...].reshape(rows_all, bp), tok[...].reshape(rows_all, dp)).astype(BF)
+
+        def finish_rows(s):
+            res_o[s] = (mix[s] + ex_sum(1, s)).astype(BF)
+
+        hops = [
+            remote(lg, lr.at[k], ln_sem.at[6 + 2 * k], ln_sem.at[7 + 2 * k], dev)
+            for k, dev in enumerate((core_dev, x_dev, y_dev))
+        ]
+
+        def ln_add(k):
+            hops[k].wait()
+            lg[...] = lg[...] + lr[k]
+
+        def ln_line(k):
+            return remote(lg, lz.at[k - 1], ln_sem.at[11 + k], ln_sem.at[14 + k], others[k - 1])
+
+        def ln_send():
+            for k in range(1, NZ):
+                send(lambda k=k: ln_line(k))
+
+        def ln_total():
+            for k in range(1, NZ):
+                ln_line(k).wait_recv()
+            total = lg[...] + lz[0] + lz[1] + lz[2]
+            for j in range(NZ):
+                @pl.when(z == j)
+                def _(j=j):
+                    gln_o[:, 0:blk] = total[:, bp * j : bp * j + blk]
+
+        ag_forward("q", 1)
+        xg_forward(tok, 0, 0, track=False)
+        ag_start("f")
+        xg_finish(tok, 0, 0)
+        ag_forward("q", 2)
+        xg_forward(tok, 0, 1, track=False)
+        xg_finish(tok, 0, 1)
+        ag_forward("o", 1)
+        ag_forward("q", 3)
+        ln_first(0)
+        ln_first(1)
+        ag_forward("o", 2)
+        ag_start("p")
+        ag_forward("o", 3)
+        ag_finish("q")
+        project(1)
+        ag_forward("f", 1)
+        project(0)
+        attend(0)
+        ag_finish("o")
+        matmul_part(att, wo, 0, False, 0)
+        ex_a(0, 0).start()
+        attend(1)
+        matmul_part(att, wo, 1, False, 0)
+        ex_a(0, 1).start()
+        ag_forward("f", 2)
+        xg_forward(dys, 1, 1)
+        ex_relay(0, 0)
+        ex_a(0, 1).wait_send()
+        ex_relay(0, 1)
+        mid(0)
+        xg_forward(dys, 1, 0)
+        xg_sent(tok, 0, 1)
+        ag_forward("f", 3)
+        ag_forward("p", 1)
+        ag_forward("p", 2)
+        xg_finish(dys, 1, 1)
+        mid(1)
+        xg_forward(sec, 2, 0)
+        xg_forward(sec, 2, 1)
+        xg_sent(tok, 0, 0)
+        ag_finish("f")
+        xg_finish(dys, 1, 0)
+        xg_finish(sec, 2, 1)
+        xg_finish(sec, 2, 0)
+        expand(1)
+        expand(0)
+        ag_forward("p", 3)
+        grad_of(gp, act, dys)
+        rs_stage("p", 3, 0)
+        ag_finish("p")
+        rs_stage("p", 0, 0)
+        rs_stage("p", 2, 0)
+        rs_stage("p", 1, 0)
+        back_act(0)
+        ex_a(0, 0).wait_send()
+        matmul_part(gel, wf, 0, True, 2)
+        ex_a(2, 0).start()
+        back_act(1)
+        ex_b(0, 0).wait_send()
+        ex_relay(2, 0)
+        matmul_part(gel, wf, 1, True, 2)
+        ex_a(2, 1).start()
+        ex_b(0, 1).wait_send()
+        ex_relay(2, 1)
+        grad_of(gf, sec, gel)
+        rs_start("f")
+        rs_stage("p", 3, 1)
+        back_mid(0)
+        back_mid(1)
+        xg_forward(tok, 3, 0)
+        rs_stage("p", 0, 1)
+        xg_finish(tok, 3, 0)
+        back_attend(0)
+        xg_forward(tok, 3, 1)
+        xg_finish(tok, 3, 1)
+        back_attend(1)
+        grad_of(gq, first, dqkv)
+        rs_start("q")
+        grad_out()
+        rs_start("o")
+        rs_stage("p", 1, 1)
+        rs_stage("p", 2, 1)
+        matmul_part(act, wp, 0, False, 1)
+        ex_a(1, 0).start()
+        matmul_part(act, wp, 1, False, 1)
+        ex_a(1, 1).start()
+        rs_stage("p", 3, 2)
+        rs_stage("p", 0, 2)
+        rs_stage("f", 3, 0)
+        ex_relay(1, 0)
+        ex_relay(1, 1)
+        ex_a(2, 0).wait_send()
+        matmul_part(dqkv, wq, 0, True, 3)
+        ex_a(3, 0).start()
+        ex_a(2, 1).wait_send()
+        matmul_part(dqkv, wq, 1, True, 3)
+        ex_a(3, 1).start()
+        rs_stage("f", 0, 0)
+        rs_stage("f", 2, 0)
+        rs_stage("f", 1, 0)
+        ex_b(2, 0).wait_send()
+        ex_relay(3, 0)
+        ex_b(2, 1).wait_send()
+        ex_relay(3, 1)
+        rs_stage("q", 3, 0)
+        rs_line("p")
+        rs_stage("q", 0, 0)
+        rs_stage("f", 3, 1)
+        rs_stage("f", 0, 1)
+        rs_stage("q", 2, 0)
+        rs_stage("f", 2, 1)
+        rs_stage("q", 1, 0)
+        rs_stage("q", 3, 1)
+        rs_stage("q", 0, 1)
+        rs_stage("f", 1, 1)
+        rs_stage("f", 3, 2)
+        rs_stage("f", 0, 2)
+        rs_stage("q", 2, 1)
+        rs_stage("q", 1, 1)
+        rs_final("p")
+        fin_start("p")
+        rs_stage("q", 3, 2)
+        rs_stage("q", 0, 2)
+        back_first(0)
+        back_first(1)
+        hops[0].start()
+        rs_final("f")
+        fin_start("f")
+        rs_final("q")
+        fin_start("q")
+        rs_stage("o", 0, 0)
+        ln_add(0)
+        hops[1].start()
+        fin_forward_y("p")
+        fin_forward_x("p", False)
+        finish_rows(0)
+        finish_rows(1)
+        rs_stage("o", 0, 1)
+        ln_add(1)
+        hops[2].start()
+        fin_forward_x("p", True)
+        rs_stage("o", 0, 2)
+        rs_final("o")
+        fin_start("o")
+        fin_forward_y("f")
+        fin_forward_x("f", False)
+        ln_add(2)
+        ln_send()
+        fin_forward_y("q")
+        fin_forward_x("q", False)
+        fin_forward_y("o")
+        fin_forward_x("o", False)
+        fin_forward_x("f", True)
+        fin_forward_x("q", True)
+        fin_forward_x("o", True)
+        ln_total()
+        for name in ("p", "f", "o", "q"):
+            fin_finish(name)
+        for s in range(WAVES):
+            for e in (1, 3):
+                ex_a(e, s).wait_send()
+                ex_b(e, s).wait_send()
+        for cond, make in ends:
+            if cond is None:
+                make().wait_send()
+            else:
+                pl.when(cond())(lambda make=make: make().wait_send())
+
+    pl.run_scoped(main, pltpu.VMEM((NB, SEQ, dp), BF), pltpu.VMEM((NB, nh * SEQ, SEQ), F32))
 
 
 def layer_call(dim, ff, tokens, cot, w_qkv, w_out, w_fc, w_proj, lengths, norms):
@@ -785,21 +859,21 @@
     nq = up128(3 * blk)
     vm, dma = pltpu.VMEM, pltpu.SemaphoreType.DMA
     big = (NB, SEQ, dp)
+    half = lambda k: (1 if k in ZFIRST else NZ, hb, nq if k == "q" else dp)
+    line = lambda k: (NZ + 1, bp if k in ZFIRST else hb, nq if k == "q" else dp)
     scratch = [
         vm(big, BF), vm(big, BF), vm((WAVES, SEQ, dp), BF),
         vm((dp, nq), BF), vm((bp, dp), BF), vm((dp, dp), BF), vm((dp, dp), BF),
-        vm(big, BF),
         vm((NB, SEQ, bp), BF), vm((NB, SEQ, bp), BF), vm((NB, SEQ, bp), BF),
-        vm((NB, (HEADS // NT) * SEQ, SEQ), F32),
         vm((NB, SEQ, bp), BF),
-        vm(big, BF),
+        vm(big, BF), vm(big, BF),
         vm((2, WAVES, 2, SEQ, dp), BF), vm((2, WAVES, SEQ, dp), BF), vm((2, WAVES, SEQ, dp), BF),
         vm((WAVES, SEQ, dp), F32), vm((WAVES, SEQ, dp), F32),
         vm(big, BF), vm(big, BF), vm(big, BF),
         vm((NB, SEQ, bp), BF), vm((NB, SEQ, nq), BF),
         vm((dp, nq), BF), vm((bp, dp), BF), vm((dp, dp), BF), vm((dp, dp), BF),
-        vm((NZ, hb, nq), BF), vm((1, hb, dp), BF), vm((NZ, hb, dp), BF), vm((NZ, hb, dp), BF),
-        vm((NZ + 1, hb, nq), BF), vm((2, hb, dp), BF), vm((NZ + 1, hb, dp), BF), vm((NZ + 1, hb, dp), BF),
+        vm(half("q"), BF), vm((1, hb, dp), BF), vm(half("f"), BF), vm(half("p"), BF),
+        vm(line("q"), BF), vm((2, hb, dp), BF), vm(line("f"), BF), vm(line("p"), BF),
         vm((8, up128(blk)), F32), vm((NZ, 8, up128(blk)), F32), vm((8, dp), F32), vm((NB, 8, SEQ), F32),
         vm((8, dp), F32), vm((3, 8, dp), F32), vm((3, 8, dp), F32),
         dma((6,)), dma((17, 5)), dma((4, 17)), dma((4, 16)), dma((8, 6)), dma((8, 4)), dma((18,)),

time: 273 us -> 257 us (0.941); the launches traced: 272 us -> 252 us
  Pallas kernels: 272 us -> 251 us
    pallas_call x1, Pallas kernels: 261 us -> 240 us  [layer_call(): pl.pallas_call(body, out_shape=(shape((WAVES, SEQ, dp), BF), shape((WAVES...]
where the time goes in v4:
time: 257 us; the launch traced here: 252 us
  Pallas kernels  251 us (98%)
    pallas_call x1, Pallas kernels, layer_call(): pl.pallas_call(body, out_shape=(shape((WAVES, SEQ, dp), BF), shape((WAVES...  240 us
    pallas_call x1, Pallas kernels, finish_call(): pl.pallas_call(lambda *refs: finish_kernel(dim, ff, *refs), grid=(blk //...  11.1 us

profile of v4, /device:TPU:0, one launch (start us, length us, event | category | flops | bytes accessed | tf_op | source)
XLA Modules:
  0.0 252.2 jit_solution(9521920074343933896)
XLA Ops:
  0.6 240.3 %shard_map.186 = (bf16[2,128,1152]{2,1,0:T(8,128)(2,1)}, bf16[2,128,1152]{2,1,0:T(8,128)(2,1)}, bf16[8,144,896]{2,1,0:T(8,128)(2,1)}, bf16[2,144,1152]{2,1,0:T(8...) custom-call(bf16[2,1120,128]{2,1,0:T(8,128)(2,1)} %bitcast.13, ...), custom_call_target="tpu_custom_call" | custom-call | tf_op jit(solution)/shard_map/pallas_call | solution.py:888
  240.9 11.1 %shard_map.187 = (bf16[2,1120,128]{2,1,0:T(8,128)(2,1)}, bf16[2,1120,128]{2,1,0:T(8,128)(2,1)}, f32[280,3360]{1,0:T(8,128)}, f32[280,1120]{1,0:T(8,128)}, f32[28...) custom-call(bf16[2,128,1152]{2,1,0:T(8,128)(2,1)} %get-tuple-element.2, ...), custom_call_target="tpu_custom_call" | custom-call | tf_op jit(solution)/shard_map/pallas_call | solution.py:940

commit v5 on v4

--- a/solution.py
+++ b/solution.py
@@ -20,6 +20,7 @@
 NB = NT * WAVES
 GELU_C = math.sqrt(2.0 / math.pi)
 GELU_A = 0.044715
+YWAY = ("f",)
 ZFIRST = ("p",)
 
 
@@ -106,11 +107,12 @@
         return pl.ds(pl.multiple_of(bp * s + hb * yy + r0, 16), hb if nr is None else nr)
 
     q_pieces = [(0, 80), (80, hb - 80)]
+    o_pieces = [(0, 48), (48, 48), (96, hb - 96)]
     gathers = {
         "q": (wq, 0, q_pieces),
         "f": (wf, 4 * len(q_pieces), [(0, hb)]),
         "p": (wp, 4 * len(q_pieces) + 4, [(0, hb)]),
-        "o": (wo, 4 * len(q_pieces) + 8, [(0, hb)]),
+        "o": (wo, 4 * len(q_pieces) + 8, o_pieces),
     }
 
     def ag_view(name, s, yy, piece):
@@ -122,7 +124,7 @@
 
     def ag_id(name, s, piece):
         ref, base, pieces = gathers[name]
-        return base if name == "o" else base + 4 * piece + s
+        return base + piece if name == "o" else base + 4 * piece + s
 
     def ag_z(name, s, piece, up):
         v = ag_view(name, s, y, piece)
@@ -227,19 +229,26 @@
     def rs_y(name, d):
         g, yr, zr, i = reduces[name]
         if name == "o":
-            return remote(g.at[rows_of(0, 1 - y)], yr.at[0], rs_sem.at[i, 0], rs_sem.at[i, 4], y_dev)
+            r0, nr = o_pieces[d]
+            return remote(
+                g.at[rows_of(0, 1 - y, r0, nr)], yr.at[0, pl.ds(r0, nr)], rs_sem.at[i, d], rs_sem.at[i, 4 + d], y_dev
+            )
         if name in ZFIRST:
             return remote(g.at[rows_of(z, 1 - y)], yr.at[0], rs_sem.at[i, 0], rs_sem.at[i, 4], y_dev)
         return remote(g.at[rows_of(d, 1 - y)], yr.at[d], rs_sem.at[i, d], rs_sem.at[i, 4 + d], y_dev)
 
     def rs_z(name, d, slot, up):
         g, yr, zr, i = reduces[name]
-        dd = 0 if name == "o" else d
+        if name == "o":
+            rows = pl.ds(*o_pieces[d])
+            return remote(
+                yr.at[0, rows], zr.at[slot, rows], rs_sem.at[i, 8 + d], rs_sem.at[i, 12 + 2 * d + slot], up_dev if up else down_dev
+            )
         if name in ZFIRST:
             return remote(
                 g.at[pl.ds(bp * d, bp)], zr.at[slot], rs_sem.at[i, 8 + d], rs_sem.at[i, 12 + slot], up_dev if up else down_dev
             )
-        return remote(yr.at[dd], zr.at[slot], rs_sem.at[i, 8 + dd], rs_sem.at[i, 12 + slot], up_dev if up else down_dev)
+        return remote(yr.at[d], zr.at[slot], rs_sem.at[i, 8 + d], rs_sem.at[i, 12 + slot], up_dev if up else down_dev)
 
     def add_up(dst, srcs):
         step = 48
@@ -255,7 +264,7 @@
         lax.fori_loop(0, dst.shape[0] // step, body, 0)
 
     def rs_start(name, dests=(3, 0, 2, 1)):
-        for d in (0,) if name == "o" else dests:
+        for d in range(len(o_pieces)) if name == "o" else dests:
             send(lambda d=d: rs_y(name, d))
 
     def rs_stage(name, d, j):
@@ -270,13 +279,15 @@
                         add_up(own, [own, zr.at[d]])
                     return
                 rs_y(name, d).wait_recv()
-                own = g.at[rows_of(0 if name == "o" else d, y)]
-                mine = yr.at[0 if name == "o" else d]
+                if name == "o":
+                    r0, nr = o_pieces[d]
+                    own, mine, past = g.at[rows_of(0, y, r0, nr)], yr.at[0, pl.ds(r0, nr)], zr.at[0, pl.ds(r0, nr)]
+                else:
+                    own, mine, past = g.at[rows_of(d, y)], yr.at[d], zr.at[d]
                 srcs = [own, mine]
-                slot = 0 if name == "o" else d
                 if j > 0:
-                    rs_z(name, d, slot, up).wait_recv()
-                    srcs.append(zr.at[slot])
+                    rs_z(name, d, 0 if name == "o" else d, up).wait_recv()
+                    srcs.append(past)
                 add_up(mine, srcs)
 
             nxt = pos + 1 if up else pos - 1
@@ -285,10 +296,10 @@
                 cond = both(z == pos, (t > pos) if up else (t < pos))
                 pl.when(cond)(run)
                 if up:
-                    send(lambda: rs_z(name, 0, 1, True), lambda: both(cond, last))
-                    send(lambda: rs_z(name, 0, 0, True), lambda: both(cond, jnp.logical_not(last)))
+                    send(lambda: rs_z(name, d, 1, True), lambda: both(cond, last))
+                    send(lambda: rs_z(name, d, 0, True), lambda: both(cond, jnp.logical_not(last)))
                 else:
-                    send(lambda: rs_z(name, 0, 0, False), lambda: cond)
+                    send(lambda: rs_z(name, d, 0, False), lambda: cond)
             else:
                 cond = z == pos
                 pl.when(cond)(run)
@@ -334,13 +345,17 @@
 
         def run(has_above, has_below):
             def go_():
-                rs_y(name, me).wait_recv()
+                parts = range(len(o_pieces)) if out else [me]
+                for d in parts:
+                    rs_y(name, d).wait_recv()
                 srcs = [g.at[rows_of(me, y)], yr.at[me]]
                 if has_above:
-                    rs_z(name, me, above, True).wait_recv()
+                    for d in parts:
+                        rs_z(name, d, above, True).wait_recv()
                     srcs.append(zr.at[above])
                 if has_below:
-                    rs_z(name, me, below, True).wait_recv()
+                    for d in parts:
+                        rs_z(name, d, below, True).wait_recv()
                     srcs.append(zr.at[below])
                 add_up(yr.at[me], srcs)
             return go_
@@ -381,18 +396,17 @@
     def fin_wait(name, tt, yy):
         fin_copy(name, fin_view(name, tt, yy), tt, yy, 0, core_dev).wait_recv()
 
-    def fin_forward_y(name):
-        here = (t == z) if name == "o" else (z >= 0)
-        pl.when(here)(lambda: fin_wait(name, t, 1 - y))
-        v = fin_view(name, t, 1 - y)
-        send(lambda: fin_copy(name, v, t, 1 - y, 3, x_dev), lambda: here)
-        send(lambda: fin_copy(name, v, t, 1 - y, 4, core_dev), lambda: here)
-
-    def fin_forward_x(name, other):
-        here = (tx == z) if name == "o" else (z >= 0)
-        for k, yy in ((6, 1 - y) if other else (5, y),):
-            pl.when(here)(lambda yy=yy: fin_wait(name, tx, yy))
-            send(lambda k=k, yy=yy: fin_copy(name, fin_view(name, tx, yy), tx, yy, k, core_dev), lambda: here)
+    def fin_forward(name, turn):
+        steps = [(t, 1 - y, x_dev), (tx, y, None), (tx, 1 - y, None)]
+        if name in YWAY:
+            steps = [(tx, y, y_dev), (t, 1 - y, None), (tx, 1 - y, None)]
+        tt, yy, dev = steps[turn]
+        here = (tt == z) if name == "o" else (z >= 0)
+        v = fin_view(name, tt, yy)
+        pl.when(here)(lambda: fin_wait(name, tt, yy))
+        if dev is not None:
+            send(lambda: fin_copy(name, v, tt, yy, 3, dev), lambda: here)
+        send(lambda: fin_copy(name, v, tt, yy, 4 + turn, core_dev), lambda: here)
 
     def fin_finish(name):
         if name == "o":
@@ -680,161 +694,167 @@
                     gln_o[:, 0:blk] = total[:, bp * j : bp * j + blk]
 
         ag_forward("q", 1)
+        ag_forward("q", 2)
+        ag_forward("q", 3)
+        ag_forward("o", 1)
+        ag_start("f")
         xg_forward(tok, 0, 0, track=False)
-        ag_start("f")
         xg_finish(tok, 0, 0)
-        ag_forward("q", 2)
+        ln_first(0)
+        ag_forward("o", 2)
         xg_forward(tok, 0, 1, track=False)
+        xg_sent(tok, 0, 0)
         xg_finish(tok, 0, 1)
-        ag_forward("o", 1)
-        ag_forward("q", 3)
-        ln_first(0)
+        xg_forward(dys, 1, 0)
         ln_first(1)
-        ag_forward("o", 2)
+        ag_forward("o", 3)
+        xg_finish(dys, 1, 0)
+        ag_forward("f", 1)
+        xg_sent(tok, 0, 1)
         ag_start("p")
-        ag_forward("o", 3)
+        xg_forward(dys, 1, 1)
         ag_finish("q")
-        project(1)
-        ag_forward("f", 1)
         project(0)
         attend(0)
+        project(1)
         ag_finish("o")
+        attend(1)
         matmul_part(att, wo, 0, False, 0)
         ex_a(0, 0).start()
-        attend(1)
+        ag_forward("f", 2)
+        ex_relay(0, 0)
+        ag_forward("p", 1)
         matmul_part(att, wo, 1, False, 0)
         ex_a(0, 1).start()
-        ag_forward("f", 2)
-        xg_forward(dys, 1, 1)
-        ex_relay(0, 0)
-        ex_a(0, 1).wait_send()
         ex_relay(0, 1)
+        ag_forward("f", 3)
         mid(0)
-        xg_forward(dys, 1, 0)
-        xg_sent(tok, 0, 1)
-        ag_forward("f", 3)
-        ag_forward("p", 1)
+        ex_b(0, 1).wait_send()
+        xg_forward(sec, 2, 0)
         ag_forward("p", 2)
         xg_finish(dys, 1, 1)
+        ex_b(0, 0).wait_send()
         mid(1)
-        xg_forward(sec, 2, 0)
-        xg_forward(sec, 2, 1)
-        xg_sent(tok, 0, 0)
+        ex_a(0, 1).wait_send()
+        ex_a(0, 0).wait_send()
         ag_finish("f")
-        xg_finish(dys, 1, 0)
-        xg_finish(sec, 2, 1)
         xg_finish(sec, 2, 0)
-        expand(1)
         expand(0)
         ag_forward("p", 3)
+        xg_forward(sec, 2, 1)
+        xg_finish(sec, 2, 1)
+        expand(1)
         grad_of(gp, act, dys)
+        ag_finish("p")
         rs_stage("p", 3, 0)
-        ag_finish("p")
         rs_stage("p", 0, 0)
-        rs_stage("p", 2, 0)
+        back_act(1)
         rs_stage("p", 1, 0)
         back_act(0)
-        ex_a(0, 0).wait_send()
         matmul_part(gel, wf, 0, True, 2)
         ex_a(2, 0).start()
-        back_act(1)
-        ex_b(0, 0).wait_send()
+        grad_of(gf, sec, gel)
+        rs_start("f")
         ex_relay(2, 0)
+        matmul_part(act, wp, 1, False, 1)
+        ex_a(1, 1).start()
         matmul_part(gel, wf, 1, True, 2)
         ex_a(2, 1).start()
-        ex_b(0, 1).wait_send()
+        back_mid(0)
         ex_relay(2, 1)
-        grad_of(gf, sec, gel)
-        rs_start("f")
-        rs_stage("p", 3, 1)
-        back_mid(0)
-        back_mid(1)
+        matmul_part(act, wp, 0, False, 1)
+        ex_a(1, 0).start()
+        rs_stage("p", 2, 0)
+        rs_stage("f", 0, 0)
+        ex_a(2, 1).wait_send()
         xg_forward(tok, 3, 0)
         rs_stage("p", 0, 1)
+        back_mid(1)
+        ex_a(2, 0).wait_send()
+        ex_relay(1, 0)
+        rs_stage("f", 3, 0)
         xg_finish(tok, 3, 0)
         back_attend(0)
+        rs_stage("p", 3, 1)
         xg_forward(tok, 3, 1)
         xg_finish(tok, 3, 1)
         back_attend(1)
         grad_of(gq, first, dqkv)
+        rs_stage("f", 2, 0)
         rs_start("q")
-        grad_out()
-        rs_start("o")
         rs_stage("p", 1, 1)
         rs_stage("p", 2, 1)
-        matmul_part(act, wp, 0, False, 1)
-        ex_a(1, 0).start()
-        matmul_part(act, wp, 1, False, 1)
-        ex_a(1, 1).start()
+        ex_b(2, 0).wait_send()
+        grad_out()
+        rs_stage("f", 0, 1)
+        ex_relay(1, 1)
+        rs_stage("f", 3, 1)
+        rs_stage("p", 0, 2)
+        matmul_part(dqkv, wq, 1, True, 3)
+        ex_a(3, 1).start()
+        rs_stage("f", 1, 0)
+        ex_b(2, 1).wait_send()
         rs_stage("p", 3, 2)
-        rs_stage("p", 0, 2)
-        rs_stage("f", 3, 0)
-        ex_relay(1, 0)
-        ex_relay(1, 1)
-        ex_a(2, 0).wait_send()
         matmul_part(dqkv, wq, 0, True, 3)
         ex_a(3, 0).start()
-        ex_a(2, 1).wait_send()
-        matmul_part(dqkv, wq, 1, True, 3)
-        ex_a(3, 1).start()
-        rs_stage("f", 0, 0)
-        rs_stage("f", 2, 0)
-        rs_stage("f", 1, 0)
-        ex_b(2, 0).wait_send()
+        rs_stage("f", 2, 1)
+        rs_stage("q", 0, 0)
         ex_relay(3, 0)
-        ex_b(2, 1).wait_send()
+        rs_stage("f", 0, 2)
+        rs_stage("q", 3, 0)
+        finish_rows(0)
+        rs_line("p")
         ex_relay(3, 1)
-        rs_stage("q", 3, 0)
-        rs_line("p")
-        rs_stage("q", 0, 0)
-        rs_stage("f", 3, 1)
-        rs_stage("f", 0, 1)
         rs_stage("q", 2, 0)
-        rs_stage("f", 2, 1)
-        rs_stage("q", 1, 0)
+        rs_stage("f", 3, 2)
+        rs_start("o")
+        back_first(0)
         rs_stage("q", 3, 1)
         rs_stage("q", 0, 1)
+        rs_stage("q", 2, 1)
+        finish_rows(1)
         rs_stage("f", 1, 1)
-        rs_stage("f", 3, 2)
-        rs_stage("f", 0, 2)
-        rs_stage("q", 2, 1)
-        rs_stage("q", 1, 1)
+        back_first(1)
+        rs_stage("q", 1, 0)
         rs_final("p")
+        hops[0].start()
         fin_start("p")
         rs_stage("q", 3, 2)
+        rs_final("f")
+        rs_stage("o", 0, 0)
+        rs_stage("q", 1, 1)
+        rs_stage("o", 0, 1)
+        rs_stage("o", 1, 0)
+        rs_stage("o", 2, 0)
+        ln_add(0)
         rs_stage("q", 0, 2)
-        back_first(0)
-        back_first(1)
-        hops[0].start()
-        rs_final("f")
+        hops[1].start()
         fin_start("f")
         rs_final("q")
+        fin_forward("p", 0)
+        ln_add(1)
+        rs_stage("o", 1, 1)
         fin_start("q")
-        rs_stage("o", 0, 0)
-        ln_add(0)
-        hops[1].start()
-        fin_forward_y("p")
-        fin_forward_x("p", False)
-        finish_rows(0)
-        finish_rows(1)
-        rs_stage("o", 0, 1)
-        ln_add(1)
-        hops[2].start()
-        fin_forward_x("p", True)
-        rs_stage("o", 0, 2)
         rs_final("o")
         fin_start("o")
-        fin_forward_y("f")
-        fin_forward_x("f", False)
+        rs_stage("o", 2, 1)
+        hops[2].start()
+        rs_stage("o", 0, 2)
+        rs_stage("o", 1, 2)
+        fin_forward("o", 0)
+        rs_stage("o", 2, 2)
+        fin_forward("f", 0)
+        fin_forward("f", 1)
+        fin_forward("q", 0)
+        fin_forward("p", 1)
         ln_add(2)
         ln_send()
-        fin_forward_y("q")
-        fin_forward_x("q", False)
-        fin_forward_y("o")
-        fin_forward_x("o", False)
-        fin_forward_x("f", True)
-        fin_forward_x("q", True)
-        fin_forward_x("o", True)
+        fin_forward("q", 1)
+        fin_forward("p", 2)
+        fin_forward("o", 2)
+        fin_forward("f", 2)
+        fin_forward("o", 1)
+        fin_forward("q", 2)
         ln_total()
         for name in ("p", "f", "o", "q"):
             fin_finish(name)
@@ -876,7 +896,7 @@
         vm(line("q"), BF), vm((2, hb, dp), BF), vm(line("f"), BF), vm(line("p"), BF),
         vm((8, up128(blk)), F32), vm((NZ, 8, up128(blk)), F32), vm((8, dp), F32), vm((NB, 8, SEQ), F32),
         vm((8, dp), F32), vm((3, 8, dp), F32), vm((3, 8, dp), F32),
-        dma((6,)), dma((17, 5)), dma((4, 17)), dma((4, 16)), dma((8, 6)), dma((8, 4)), dma((18,)),
+        dma((6,)), dma((19, 5)), dma((4, 18)), dma((4, 16)), dma((8, 6)), dma((8, 4)), dma((18,)),
     ]
     hbm = pl.BlockSpec(memory_space=pl.ANY)
     inv = pl.BlockSpec(memory_space=pltpu.VMEM)

time: 257 us -> 231 us (0.90); the launches traced: 252 us -> 230 us
  Pallas kernels: 251 us -> 229 us
    pallas_call x1, Pallas kernels: 240 us -> 218 us  [layer_call(): pl.pallas_call(body, out_shape=(shape((WAVES, SEQ, dp), BF), shape((WAVES...]
where the time goes in v5:
time: 231 us; the launch traced here: 230 us
  Pallas kernels  229 us (99%)
    pallas_call x1, Pallas kernels, layer_call(): pl.pallas_call(body, out_shape=(shape((WAVES, SEQ, dp), BF), shape((WAVES...  218 us
    pallas_call x1, Pallas kernels, finish_call(): pl.pallas_call(lambda *refs: finish_kernel(dim, ff, *refs), grid=(blk //...  11.1 us

profile of v5, /device:TPU:0, one launch (start us, length us, event | category | flops | bytes accessed | tf_op | source)
XLA Modules:
  0.0 229.5 jit_solution(2635088126955384099)
XLA Ops:
  0.6 217.6 %shard_map.186 = (bf16[2,128,1152]{2,1,0:T(8,128)(2,1)}, bf16[2,128,1152]{2,1,0:T(8,128)(2,1)}, bf16[8,144,896]{2,1,0:T(8,128)(2,1)}, bf16[2,144,1152]{2,1,0:T(8...) custom-call(bf16[2,1120,128]{2,1,0:T(8,128)(2,1)} %bitcast.13, ...), custom_call_target="tpu_custom_call" | custom-call | tf_op jit(solution)/shard_map/pallas_call | solution.py:908
  218.2 11.1 %shard_map.187 = (bf16[2,1120,128]{2,1,0:T(8,128)(2,1)}, bf16[2,1120,128]{2,1,0:T(8,128)(2,1)}, f32[280,3360]{1,0:T(8,128)}, f32[280,1120]{1,0:T(8,128)}, f32[28...) custom-call(bf16[2,128,1152]{2,1,0:T(8,128)(2,1)} %get-tuple-element.2, ...), custom_call_target="tpu_custom_call" | custom-call | tf_op jit(solution)/shard_map/pallas_call | solution.py:960

commit v6 on v5

--- a/solution.py
+++ b/solution.py
@@ -20,7 +20,7 @@
 NB = NT * WAVES
 GELU_C = math.sqrt(2.0 / math.pi)
 GELU_A = 0.044715
-YWAY = ("f",)
+YWAY = ("f", "q",)
 ZFIRST = ("p",)
 
 
@@ -101,7 +101,6 @@
     others = [(w, lax.rem(z + k, NZ)) for k in range(1, NZ)]
     for dev in [core_dev, x_dev, y_dev] + others:
         pl.semaphore_signal(barrier, inc=1, device_id=dev, device_id_type=MESH)
-    pl.semaphore_wait(barrier, 3 + len(others))
 
     def rows_of(s, yy, r0=0, nr=None):
         return pl.ds(pl.multiple_of(bp * s + hb * yy + r0, 16), hb if nr is None else nr)
@@ -420,12 +419,14 @@
                     fin_wait(name, 2 * xx + (1 - c), yy)
             keep_own(name).wait()
 
-    def prepare(rq, rt, ro, rd, turned):
+    def prepare(rq, rt, ro, rd, turned, rf, rp):
         loads = [
             pltpu.make_async_copy(wq_h, rq, raw_sem.at[0]),
             pltpu.make_async_copy(tok_h, rt, raw_sem.at[1]),
             pltpu.make_async_copy(wo_h, ro, raw_sem.at[2]),
             pltpu.make_async_copy(dy_h, rd, raw_sem.at[3]),
+            pltpu.make_async_copy(wf_h, rf, raw_sem.at[4]),
+            pltpu.make_async_copy(wp_h.at[pl.ds(pl.multiple_of(blk * t, 8), blk)], rp, raw_sem.at[5]),
         ]
         for load in loads:
             load.start()
@@ -433,8 +434,6 @@
         for k, ref in enumerate((g1_i, b1_i, g2_i, b2_i)):
             lnv[k : k + 1, 0:blk] = ref[...].astype(F32).reshape(1, blk)
         lnr[z] = lnv[...]
-        for k in range(1, NZ):
-            send(lambda k=k: remote(lnv, lnr.at[z], ln_sem.at[k - 1], ln_sem.at[2 + k], others[k - 1]))
 
         loads[0].wait()
         wq[pl.ds(base, bp), :] = jnp.zeros((bp, nq), BF)
@@ -443,7 +442,10 @@
             def _(k=k):
                 for j in range(3):
                     wq[pl.ds(base, blk), blk * j : blk * (j + 1)] = rq[:, dim * j + blk * k : dim * j + blk * (k + 1)]
+        pl.semaphore_wait(barrier, 3 + len(others))
         ag_start("q")
+        for k in range(1, NZ):
+            send(lambda k=k: remote(lnv, lnr.at[z], ln_sem.at[k - 1], ln_sem.at[2 + k], others[k - 1]))
 
         turned[...] = jnp.zeros_like(turned)
 
@@ -471,25 +473,21 @@
             spread(dys.at[blk_of(s, c, x)], rd.at[s])
             xg_start(dys, 1, s)
 
-    def prepare_mlp(rf, rp):
-        loads = [
-            pltpu.make_async_copy(wf_h, rf, raw_sem.at[4]),
-            pltpu.make_async_copy(wp_h.at[pl.ds(pl.multiple_of(blk * t, 8), blk)], rp, raw_sem.at[5]),
-        ]
-        for load in loads:
-            load.start()
-        loads[0].wait()
-        wf[pl.ds(base, bp), :] = jnp.zeros((bp, dp), BF)
-        for k in range(NT):
-            @pl.when(t == k)
-            def _(k=k):
-                for j in range(NZ):
-                    lo = (ff // NZ) * j + blk * k
-                    wf[pl.ds(base, blk), bp * j : bp * j + blk] = rf[:, lo : lo + blk]
-        loads[1].wait()
-        wp[pl.ds(base, bp), :] = jnp.zeros((bp, dp), BF)
-        for j in range(NZ):
-            wp[pl.ds(base, blk), bp * j : bp * j + blk] = rp[:, blk * j : blk * (j + 1)]
+        def prepare_mlp():
+            loads[4].wait()
+            wf[pl.ds(base, bp), :] = jnp.zeros((bp, dp), BF)
+            for k in range(NT):
+                @pl.when(t == k)
+                def _(k=k):
+                    for j in range(NZ):
+                        lo = (ff // NZ) * j + blk * k
+                        wf[pl.ds(base, blk), bp * j : bp * j + blk] = rf[:, lo : lo + blk]
+            loads[5].wait()
+            wp[pl.ds(base, bp), :] = jnp.zeros((bp, dp), BF)
+            for j in range(NZ):
+                wp[pl.ds(base, blk), bp * j : bp * j + blk] = rp[:, blk * j : blk * (j + 1)]
+
+        prepare_mlp()
 
     pl.run_scoped(
         prepare,
@@ -498,8 +496,9 @@
         pltpu.VMEM((blk, dim), BF),
         pltpu.VMEM((WAVES, dim, SEQ), BF),
         pltpu.VMEM((dp, SEQ), BF),
+        pltpu.VMEM((blk, ff), BF),
+        pltpu.VMEM((blk, dim), BF),
     )
-    pl.run_scoped(prepare_mlp, pltpu.VMEM((blk, ff), BF), pltpu.VMEM((blk, dim), BF))
 
     def main(first, pm):
         for k in range(1, NZ):
@@ -603,16 +602,27 @@
                 return carry
             lax.fori_loop(0, 2, body, 0)
 
-        def grad_of(dst, left, right):
+        def grad_of(name, left, right):
+            dst = reduces[name][0]
             step = 384
             rows = NB * SEQ
-
-            def body(j, carry):
-                cols = pl.ds(pl.multiple_of(j * step, step), step)
+            leave = {} if name in ZFIRST else {0: (3,), 1: (0,), 2: (2, 1)}
+
+            def depart(k):
+                for d in leave.get(k, ()):
+                    rs_y(name, d).start()
+
+            def body(k, carry):
+                cols = pl.ds(pl.multiple_of(lax.rem(k + 2, 3) * step, step), step)
                 out = tn(left[:, :, cols].reshape(rows, step), right[...].reshape(rows, right.shape[2]))
                 dst[cols, :] = out.astype(BF)
+                for n in leave:
+                    pl.when(k == n)(lambda n=n: depart(n))
                 return carry
+
             lax.fori_loop(0, dp // step, body, 0)
+            for ds in leave.values():
+                ends.extend((None, lambda d=d: rs_y(name, d)) for d in ds)
 
         def back_act(s):
             def body(i, carry):
@@ -694,168 +704,166 @@
                     gln_o[:, 0:blk] = total[:, bp * j : bp * j + blk]
 
         ag_forward("q", 1)
+        ag_forward("o", 1)
         ag_forward("q", 2)
+        ag_forward("o", 2)
+        ag_start("f")
+        ag_start("p")
+        xg_forward(tok, 0, 0, track=False)
         ag_forward("q", 3)
-        ag_forward("o", 1)
-        ag_start("f")
-        xg_forward(tok, 0, 0, track=False)
         xg_finish(tok, 0, 0)
+        xg_forward(tok, 0, 1, track=False)
         ln_first(0)
-        ag_forward("o", 2)
-        xg_forward(tok, 0, 1, track=False)
-        xg_sent(tok, 0, 0)
         xg_finish(tok, 0, 1)
+        ln_first(1)
         xg_forward(dys, 1, 0)
-        ln_first(1)
+        xg_finish(dys, 1, 0)
         ag_forward("o", 3)
-        xg_finish(dys, 1, 0)
-        ag_forward("f", 1)
-        xg_sent(tok, 0, 1)
-        ag_start("p")
-        xg_forward(dys, 1, 1)
         ag_finish("q")
         project(0)
         attend(0)
         project(1)
+        ag_forward("f", 1)
         ag_finish("o")
-        attend(1)
         matmul_part(att, wo, 0, False, 0)
         ex_a(0, 0).start()
-        ag_forward("f", 2)
         ex_relay(0, 0)
-        ag_forward("p", 1)
+        xg_sent(tok, 0, 0)
+        attend(1)
+        xg_forward(dys, 1, 1)
         matmul_part(att, wo, 1, False, 0)
         ex_a(0, 1).start()
+        ag_forward("f", 2)
+        ag_forward("p", 1)
         ex_relay(0, 1)
+        mid(0)
         ag_forward("f", 3)
-        mid(0)
+        mid(1)
+        xg_finish(dys, 1, 1)
+        ag_forward("p", 2)
+        xg_sent(tok, 0, 1)
         ex_b(0, 1).wait_send()
+        ex_a(0, 0).wait_send()
         xg_forward(sec, 2, 0)
-        ag_forward("p", 2)
-        xg_finish(dys, 1, 1)
-        ex_b(0, 0).wait_send()
-        mid(1)
-        ex_a(0, 1).wait_send()
-        ex_a(0, 0).wait_send()
+        xg_forward(sec, 2, 1)
+        ag_forward("p", 3)
+        xg_finish(sec, 2, 0)
         ag_finish("f")
-        xg_finish(sec, 2, 0)
         expand(0)
-        ag_forward("p", 3)
-        xg_forward(sec, 2, 1)
         xg_finish(sec, 2, 1)
         expand(1)
-        grad_of(gp, act, dys)
+        grad_of("p", act, dys)
+        rs_stage("p", 2, 0)
+        ex_a(0, 1).wait_send()
+        rs_stage("p", 0, 0)
         ag_finish("p")
+        back_act(1)
+        matmul_part(gel, wf, 1, True, 2)
+        ex_a(2, 1).start()
+        back_act(0)
+        ex_relay(2, 1)
         rs_stage("p", 3, 0)
-        rs_stage("p", 0, 0)
-        back_act(1)
-        rs_stage("p", 1, 0)
-        back_act(0)
         matmul_part(gel, wf, 0, True, 2)
         ex_a(2, 0).start()
-        grad_of(gf, sec, gel)
-        rs_start("f")
+        ex_b(0, 0).wait_send()
         ex_relay(2, 0)
+        grad_of("f", sec, gel)
+        matmul_part(act, wp, 0, False, 1)
+        ex_a(1, 0).start()
+        back_mid(0)
+        rs_stage("p", 1, 0)
         matmul_part(act, wp, 1, False, 1)
         ex_a(1, 1).start()
-        matmul_part(gel, wf, 1, True, 2)
-        ex_a(2, 1).start()
-        back_mid(0)
-        ex_relay(2, 1)
-        matmul_part(act, wp, 0, False, 1)
-        ex_a(1, 0).start()
-        rs_stage("p", 2, 0)
-        rs_stage("f", 0, 0)
-        ex_a(2, 1).wait_send()
+        rs_stage("f", 3, 0)
+        back_mid(1)
+        rs_stage("p", 3, 1)
         xg_forward(tok, 3, 0)
         rs_stage("p", 0, 1)
-        back_mid(1)
-        ex_a(2, 0).wait_send()
-        ex_relay(1, 0)
-        rs_stage("f", 3, 0)
+        rs_stage("f", 0, 0)
         xg_finish(tok, 3, 0)
         back_attend(0)
-        rs_stage("p", 3, 1)
         xg_forward(tok, 3, 1)
         xg_finish(tok, 3, 1)
         back_attend(1)
-        grad_of(gq, first, dqkv)
+        grad_of("q", first, dqkv)
+        ex_a(2, 1).wait_send()
+        ex_b(2, 0).wait_send()
+        rs_stage("f", 1, 0)
+        rs_stage("p", 1, 1)
         rs_stage("f", 2, 0)
-        rs_start("q")
-        rs_stage("p", 1, 1)
+        rs_stage("p", 3, 2)
         rs_stage("p", 2, 1)
-        ex_b(2, 0).wait_send()
-        grad_out()
-        rs_stage("f", 0, 1)
-        ex_relay(1, 1)
-        rs_stage("f", 3, 1)
-        rs_stage("p", 0, 2)
+        ex_b(2, 1).wait_send()
         matmul_part(dqkv, wq, 1, True, 3)
         ex_a(3, 1).start()
-        rs_stage("f", 1, 0)
-        ex_b(2, 1).wait_send()
-        rs_stage("p", 3, 2)
+        rs_stage("p", 0, 2)
+        ex_relay(1, 0)
+        ex_a(2, 0).wait_send()
+        ex_relay(1, 1)
+        rs_stage("f", 0, 1)
         matmul_part(dqkv, wq, 0, True, 3)
         ex_a(3, 0).start()
+        ex_relay(3, 1)
+        rs_stage("q", 3, 0)
+        grad_out()
+        rs_line("p")
+        rs_stage("f", 3, 1)
+        rs_start("o")
+        ex_relay(3, 0)
+        rs_stage("q", 0, 0)
+        rs_stage("q", 2, 0)
+        rs_stage("f", 1, 1)
+        rs_stage("q", 1, 0)
         rs_stage("f", 2, 1)
-        rs_stage("q", 0, 0)
-        ex_relay(3, 0)
+        rs_final("p")
+        fin_start("p")
+        back_first(1)
+        back_first(0)
+        hops[0].start()
+        rs_stage("q", 3, 1)
+        rs_stage("f", 3, 2)
+        rs_stage("o", 1, 0)
         rs_stage("f", 0, 2)
-        rs_stage("q", 3, 0)
-        finish_rows(0)
-        rs_line("p")
-        ex_relay(3, 1)
-        rs_stage("q", 2, 0)
-        rs_stage("f", 3, 2)
-        rs_start("o")
-        back_first(0)
-        rs_stage("q", 3, 1)
         rs_stage("q", 0, 1)
+        finish_rows(1)
+        ln_add(0)
+        hops[1].start()
+        rs_stage("o", 0, 0)
+        rs_final("f")
         rs_stage("q", 2, 1)
-        finish_rows(1)
-        rs_stage("f", 1, 1)
-        back_first(1)
-        rs_stage("q", 1, 0)
-        rs_final("p")
-        hops[0].start()
-        fin_start("p")
+        fin_start("f")
+        rs_stage("q", 1, 1)
+        rs_stage("q", 0, 2)
+        rs_stage("o", 2, 0)
+        ln_add(1)
         rs_stage("q", 3, 2)
-        rs_final("f")
-        rs_stage("o", 0, 0)
-        rs_stage("q", 1, 1)
         rs_stage("o", 0, 1)
-        rs_stage("o", 1, 0)
-        rs_stage("o", 2, 0)
-        ln_add(0)
-        rs_stage("q", 0, 2)
-        hops[1].start()
-        fin_start("f")
+        hops[2].start()
         rs_final("q")
+        fin_start("q")
+        rs_stage("o", 1, 1)
         fin_forward("p", 0)
-        ln_add(1)
-        rs_stage("o", 1, 1)
-        fin_start("q")
         rs_final("o")
         fin_start("o")
         rs_stage("o", 2, 1)
-        hops[2].start()
+        fin_forward("f", 0)
+        finish_rows(0)
+        rs_stage("o", 1, 2)
+        ln_add(2)
+        ln_send()
         rs_stage("o", 0, 2)
-        rs_stage("o", 1, 2)
-        fin_forward("o", 0)
+        fin_forward("o", 1)
+        fin_forward("f", 1)
         rs_stage("o", 2, 2)
-        fin_forward("f", 0)
-        fin_forward("f", 1)
+        fin_forward("q", 1)
         fin_forward("q", 0)
         fin_forward("p", 1)
-        ln_add(2)
-        ln_send()
-        fin_forward("q", 1)
         fin_forward("p", 2)
+        fin_forward("o", 0)
+        ln_total()
+        fin_forward("f", 2)
+        fin_forward("q", 2)
         fin_forward("o", 2)
-        fin_forward("f", 2)
-        fin_forward("o", 1)
-        fin_forward("q", 2)
-        ln_total()
         for name in ("p", "f", "o", "q"):
             fin_finish(name)
         for s in range(WAVES):

time: 231 us -> 225 us (0.974)
  Pallas kernels: 229 us -> 224 us
    pallas_call x1, Pallas kernels: 218 us -> 213 us  [layer_call(): pl.pallas_call(body, out_shape=(shape((WAVES, SEQ, dp), BF), shape((WAVES...]
where the time goes in v6:
time: 225 us
  Pallas kernels  224 us (100%)
    pallas_call x1, Pallas kernels, layer_call(): pl.pallas_call(body, out_shape=(shape((WAVES, SEQ, dp), BF), shape((WAVES...  213 us
    pallas_call x1, Pallas kernels, finish_call(): pl.pallas_call(lambda *refs: finish_kernel(dim, ff, *refs), grid=(blk //...  11.1 us

profile of v6, /device:TPU:0, one launch (start us, length us, event | category | flops | bytes accessed | tf_op | source)
XLA Modules:
  0.0 224.7 jit_solution(15035402473291914613)
XLA Ops:
  0.6 212.8 %shard_map.186 = (bf16[2,128,1152]{2,1,0:T(8,128)(2,1)}, bf16[2,128,1152]{2,1,0:T(8,128)(2,1)}, bf16[8,144,896]{2,1,0:T(8,128)(2,1)}, bf16[2,144,1152]{2,1,0:T(8...) custom-call(bf16[2,1120,128]{2,1,0:T(8,128)(2,1)} %bitcast.13, ...), custom_call_target="tpu_custom_call" | custom-call | tf_op jit(solution)/shard_map/pallas_call | solution.py:916
  213.4 11.1 %shard_map.187 = (bf16[2,1120,128]{2,1,0:T(8,128)(2,1)}, bf16[2,1120,128]{2,1,0:T(8,128)(2,1)}, f32[280,3360]{1,0:T(8,128)}, f32[280,1120]{1,0:T(8,128)}, f32[28...) custom-call(bf16[2,128,1152]{2,1,0:T(8,128)(2,1)} %get-tuple-element.2, ...), custom_call_target="tpu_custom_call" | custom-call | tf_op jit(solution)/shard_map/pallas_call | solution.py:968

commit v7 on v6

--- a/solution.py
+++ b/solution.py
@@ -109,9 +109,9 @@
     o_pieces = [(0, 48), (48, 48), (96, hb - 96)]
     gathers = {
         "q": (wq, 0, q_pieces),
-        "f": (wf, 4 * len(q_pieces), [(0, hb)]),
-        "p": (wp, 4 * len(q_pieces) + 4, [(0, hb)]),
-        "o": (wo, 4 * len(q_pieces) + 8, o_pieces),
+        "f": (wf, 8, q_pieces),
+        "p": (wp, 16, q_pieces),
+        "o": (wo, 24, o_pieces),
     }
 
     def ag_view(name, s, yy, piece):
@@ -443,9 +443,9 @@
                 for j in range(3):
                     wq[pl.ds(base, blk), blk * j : blk * (j + 1)] = rq[:, dim * j + blk * k : dim * j + blk * (k + 1)]
         pl.semaphore_wait(barrier, 3 + len(others))
-        ag_start("q")
         for k in range(1, NZ):
             send(lambda k=k: remote(lnv, lnr.at[z], ln_sem.at[k - 1], ln_sem.at[2 + k], others[k - 1]))
+        ag_start("q")
 
         turned[...] = jnp.zeros_like(turned)
 
@@ -501,11 +501,13 @@
     )
 
     def main(first, pm):
-        for k in range(1, NZ):
-            remote(lnv, lnr.at[lax.rem(z + NZ - k, NZ)], ln_sem.at[k - 1], ln_sem.at[2 + k], others[k - 1]).wait_recv()
-        vec[...] = jnp.zeros_like(vec)
-        for j in range(NZ):
-            vec[:, bp * j : bp * j + blk] = lnr[j, :, 0:blk]
+        def vectors():
+            for k in range(1, NZ):
+                remote(lnv, lnr.at[lax.rem(z + NZ - k, NZ)], ln_sem.at[k - 1], ln_sem.at[2 + k], others[k - 1]).wait_recv()
+            vec[...] = jnp.zeros_like(vec)
+            for j in range(NZ):
+                vec[:, bp * j : bp * j + blk] = lnr[j, :, 0:blk]
+
         lg[...] = jnp.zeros_like(lg)
         dqkv[...] = jnp.zeros_like(dqkv)
 
@@ -713,6 +715,7 @@
         ag_forward("q", 3)
         xg_finish(tok, 0, 0)
         xg_forward(tok, 0, 1, track=False)
+        vectors()
         ln_first(0)
         xg_finish(tok, 0, 1)
         ln_first(1)
@@ -721,8 +724,8 @@
         ag_forward("o", 3)
         ag_finish("q")
         project(0)
+        project(1)
         attend(0)
-        project(1)
         ag_forward("f", 1)
         ag_finish("o")
         matmul_part(att, wo, 0, False, 0)
@@ -768,10 +771,10 @@
         ex_b(0, 0).wait_send()
         ex_relay(2, 0)
         grad_of("f", sec, gel)
+        back_mid(0)
+        rs_stage("p", 1, 0)
         matmul_part(act, wp, 0, False, 1)
         ex_a(1, 0).start()
-        back_mid(0)
-        rs_stage("p", 1, 0)
         matmul_part(act, wp, 1, False, 1)
         ex_a(1, 1).start()
         rs_stage("f", 3, 0)
@@ -842,15 +845,15 @@
         rs_final("q")
         fin_start("q")
         rs_stage("o", 1, 1)
-        fin_forward("p", 0)
         rs_final("o")
         fin_start("o")
+        fin_forward("p", 0)
         rs_stage("o", 2, 1)
         fin_forward("f", 0)
         finish_rows(0)
-        rs_stage("o", 1, 2)
         ln_add(2)
         ln_send()
+        rs_stage("o", 1, 2)
         rs_stage("o", 0, 2)
         fin_forward("o", 1)
         fin_forward("f", 1)
@@ -904,7 +907,7 @@
         vm(line("q"), BF), vm((2, hb, dp), BF), vm(line("f"), BF), vm(line("p"), BF),
         vm((8, up128(blk)), F32), vm((NZ, 8, up128(blk)), F32), vm((8, dp), F32), vm((NB, 8, SEQ), F32),
         vm((8, dp), F32), vm((3, 8, dp), F32), vm((3, 8, dp), F32),
-        dma((6,)), dma((19, 5)), dma((4, 18)), dma((4, 16)), dma((8, 6)), dma((8, 4)), dma((18,)),
+        dma((6,)), dma((27, 5)), dma((4, 18)), dma((4, 16)), dma((8, 6)), dma((8, 4)), dma((18,)),
     ]
     hbm = pl.BlockSpec(memory_space=pl.ANY)
     inv = pl.BlockSpec(memory_space=pltpu.VMEM)

time: 225 us -> 223 us (level)
  Pallas kernels: 224 us -> 221 us
    pallas_call x1, Pallas kernels: 213 us -> 210 us  [layer_call(): pl.pallas_call(body, out_shape=(shape((WAVES, SEQ, dp), BF), shape((WAVES...]
where the time goes in v7:
time: 223 us; the launch traced here: 222 us
  Pallas kernels  221 us (99%)
    pallas_call x1, Pallas kernels, layer_call(): pl.pallas_call(body, out_shape=(shape((WAVES, SEQ, dp), BF), shape((WAVES...  210 us
    pallas_call x1, Pallas kernels, finish_call(): pl.pallas_call(lambda *refs: finish_kernel(dim, ff, *refs), grid=(blk //...  11.1 us

profile of v7, /device:TPU:0, one launch (start us, length us, event | category | flops | bytes accessed | tf_op | source)
XLA Modules:
  0.0 222.2 jit_solution(11983875502754308128)
XLA Ops:
  0.6 210.2 %shard_map.186 = (bf16[2,128,1152]{2,1,0:T(8,128)(2,1)}, bf16[2,128,1152]{2,1,0:T(8,128)(2,1)}, bf16[8,144,896]{2,1,0:T(8,128)(2,1)}, bf16[2,144,1152]{2,1,0:T(8...) custom-call(bf16[2,1120,128]{2,1,0:T(8,128)(2,1)} %bitcast.13, ...), custom_call_target="tpu_custom_call" | custom-call | tf_op jit(solution)/shard_map/pallas_call | solution.py:919
  210.8 11.1 %shard_map.187 = (bf16[2,1120,128]{2,1,0:T(8,128)(2,1)}, bf16[2,1120,128]{2,1,0:T(8,128)(2,1)}, f32[280,3360]{1,0:T(8,128)}, f32[280,1120]{1,0:T(8,128)}, f32[28...) custom-call(bf16[2,128,1152]{2,1,0:T(8,128)(2,1)} %get-tuple-element.2, ...), custom_call_target="tpu_custom_call" | custom-call | tf_op jit(solution)/shard_map/pallas_call | solution.py:971

commit v8 on v7

--- a/solution.py
+++ b/solution.py
@@ -756,6 +756,7 @@
         xg_finish(sec, 2, 1)
         expand(1)
         grad_of("p", act, dys)
+        rs_stage("p", 3, 0)
         rs_stage("p", 2, 0)
         ex_a(0, 1).wait_send()
         rs_stage("p", 0, 0)
@@ -765,10 +766,9 @@
         ex_a(2, 1).start()
         back_act(0)
         ex_relay(2, 1)
-        rs_stage("p", 3, 0)
+        ex_b(0, 0).wait_send()
         matmul_part(gel, wf, 0, True, 2)
         ex_a(2, 0).start()
-        ex_b(0, 0).wait_send()
         ex_relay(2, 0)
         grad_of("f", sec, gel)
         back_mid(0)
@@ -806,10 +806,10 @@
         rs_stage("f", 0, 1)
         matmul_part(dqkv, wq, 0, True, 3)
         ex_a(3, 0).start()
+        rs_line("p")
         ex_relay(3, 1)
         rs_stage("q", 3, 0)
         grad_out()
-        rs_line("p")
         rs_stage("f", 3, 1)
         rs_start("o")
         ex_relay(3, 0)

time: 223 us -> 223 us (level)
  no operation moved by 1% of the time
where the time goes in v8:
time: 223 us; the launch traced here: 222 us
  Pallas kernels  221 us (99%)
    pallas_call x1, Pallas kernels, layer_call(): pl.pallas_call(body, out_shape=(shape((WAVES, SEQ, dp), BF), shape((WAVES...  210 us
    pallas_call x1, Pallas kernels, finish_call(): pl.pallas_call(lambda *refs: finish_kernel(dim, ff, *refs), grid=(blk //...  11.1 us

profile of v8, /device:TPU:0, one launch (start us, length us, event | category | flops | bytes accessed | tf_op | source)
XLA Modules:
  0.0 222.2 jit_solution(882309768954232658)
XLA Ops:
  0.6 210.2 %shard_map.186 = (bf16[2,128,1152]{2,1,0:T(8,128)(2,1)}, bf16[2,128,1152]{2,1,0:T(8,128)(2,1)}, bf16[8,144,896]{2,1,0:T(8,128)(2,1)}, bf16[2,144,1152]{2,1,0:T(8...) custom-call(bf16[2,1120,128]{2,1,0:T(8,128)(2,1)} %bitcast.13, ...), custom_call_target="tpu_custom_call" | custom-call | tf_op jit(solution)/shard_map/pallas_call | solution.py:919
  210.8 11.1 %shard_map.187 = (bf16[2,1120,128]{2,1,0:T(8,128)(2,1)}, bf16[2,1120,128]{2,1,0:T(8,128)(2,1)}, f32[280,3360]{1,0:T(8,128)}, f32[280,1120]{1,0:T(8,128)}, f32[28...) custom-call(bf16[2,128,1152]{2,1,0:T(8,128)(2,1)} %get-tuple-element.2, ...), custom_call_target="tpu_custom_call" | custom-call | tf_op jit(solution)/shard_map/pallas_call | solution.py:971
